TPU v7x, 32 devices: a whole 2x2x4 slice. The times are simulated.
32 devices in a mesh: wide: 8 (over y, x, core), narrow: 4 (over z).
Axes of the slice: x: 2, y: 2, z: 4, core: 2. Of those that a mesh axis runs over, the one named last changes fastest.
Arguments:
- tokens: bfloat16 [16384, 1024], P(('wide', 'narrow')), may hold values from -32 to 32
- cotangent: bfloat16 [16384, 1024], P(('wide', 'narrow')), may hold values from -6 to 6
- seq_lengths: int32 [8, 3], P('wide'), may hold values from 1 to 1536, 2048 in all within a row
- step_count: int32 [1], replicated, may hold values from 6 to 20
- norm_params: float32 [2, 1024], replicated, may hold values from -1 to 4.5, as said below
- norm_first: float32 [2, 1024], replicated, may hold values from -12 to 12
- norm_second: float32 [2, 1024], replicated, may hold values from 8 to 32
- proj_weight: float32 [1024, 3072], P('narrow', 'wide'), may hold values from -0.1875 to 0.1875
- proj_first: float32 [1024, 3072], P('narrow', 'wide'), may hold values from -6 to 6
- proj_second: float32 [1024, 3072], P('narrow', 'wide'), may hold values from 2.2 to 9
- merge_weight: float32 [1024, 1024], P('narrow', 'wide'), may hold values from -0.75 to 0.75
- merge_first: float32 [1024, 1024], P('narrow', 'wide'), may hold values from -1.2 to 1.2
- merge_second: float32 [1024, 1024], P('narrow', 'wide'), may hold values from 0.09 to 0.36
- up_weight: float32 [1024, 4096], P(None, 'narrow'), may hold values from -0.1875 to 0.1875
- up_first: float32 [1024, 4096], P(None, 'narrow'), may hold values from -1.4 to 1.4
- up_second: float32 [1024, 4096], P(None, 'narrow'), may hold values from 0.12 to 0.5
- down_weight: float32 [4096, 1024], P('narrow'), may hold values from -0.09375 to 0.09375
- down_first: float32 [4096, 1024], P('narrow'), may hold values from -3.4 to 3.4
- down_second: float32 [4096, 1024], P('narrow'), may hold values from 0.7 to 2.9
Outputs:
- layer_out: bfloat16 [16384, 1024], P(('wide', 'narrow'))
- input_grad: float32 [16384, 1024], P(('wide', 'narrow'))
- grad_norm: float32 [1], replicated
- residual_rms: float32 [1], replicated
- norm_grads: float32 [2, 1024], replicated
- new_norm_params: float32 [2, 1024], replicated
- new_norm_first: float32 [2, 1024], replicated
- new_norm_second: float32 [2, 1024], replicated
- new_proj_weight: float32 [1024, 3072], P('narrow', 'wide')
- new_proj_first: float32 [1024, 3072], P('narrow', 'wide')
- new_proj_second: float32 [1024, 3072], P('narrow', 'wide')
- new_merge_weight: float32 [1024, 1024], P('narrow', 'wide')
- new_merge_first: float32 [1024, 1024], P('narrow', 'wide')
- new_merge_second: float32 [1024, 1024], P('narrow', 'wide')
- new_up_weight: float32 [1024, 4096], P(None, 'narrow')
- new_up_first: float32 [1024, 4096], P(None, 'narrow')
- new_up_second: float32 [1024, 4096], P(None, 'narrow')
- new_down_weight: float32 [4096, 1024], P('narrow')
- new_down_first: float32 [4096, 1024], P('narrow')
- new_down_second: float32 [4096, 1024], P('narrow')
- branch_norms: float32 [2], replicated
- new_proj_copy: bfloat16 [1024, 3072], P('narrow', 'wide')
- new_merge_copy: bfloat16 [1024, 1024], P('narrow', 'wide')
- new_up_copy: bfloat16 [1024, 4096], P(None, 'narrow')
- new_down_copy: bfloat16 [4096, 1024], P('narrow')
Inputs may be any that keep to these rules, and one draw needn't show every extreme that they name: `seq_lengths`: row g holds the lengths of the 3 sequences of group g, in order; they sum to 2048, and in every row the longest is exactly 1536. `norm_params`: row 0 holds the gains (positive), row 1 the biases.
All inputs are finite; a program needn't handle non-finite values.
Results may differ from a plain program's by a relative error of at most 0.02.
Values may be sent and summed in bfloat16 or wider, within the bound.
A program may use at most 320 MiB of HBM per device.

v0:
```python
from functools import partial
import math

import jax
import jax.numpy as jnp
from jax import lax
from jax.sharding import PartitionSpec as P

HEADS = 16
HEAD = 64
D = 1024
ROT = 16
SEQ_MOST = 2048
NPARAMS = 12584960


norm_eps = 1e-05
adam_eps = 1e-08
beta_first = 0.5
beta_second = 0.5
decay_rate = 0.01
matrix_rate = 0.1
norm_rate = 1.0
warmup_steps = 20.0
masked_score = -1e30


def from_behind(array, axis, by):
    count = lax.axis_size(axis)
    pairs = [(i, i + by) for i in range(count) if 0 <= i + by < count]
    return lax.ppermute(array, axis, pairs)


def locate(lengths, first_index, row_count):
    token_index = first_index + jnp.arange(row_count, dtype=jnp.int32)
    seq_ends = jnp.cumsum(lengths)
    starts = seq_ends - lengths
    segment = jnp.sum(
        (seq_ends[None, :] <= token_index[:, None]).astype(jnp.int32), axis=1, dtype=jnp.int32
    )
    choose = segment[:, None] == jnp.arange(lengths.shape[0], dtype=jnp.int32)[None, :]
    seq_start = jnp.sum(jnp.where(choose, starts[None, :], 0), axis=1, dtype=jnp.int32)
    return (segment, token_index, token_index - seq_start)


def rotary_tables(position):
    half_rot = ROT // 2
    frequency = jnp.power(10000.0, -2.0 * jnp.arange(half_rot, dtype=jnp.float32) / ROT)
    phases = position.astype(jnp.float32)[:, None] * frequency[None, :]
    return (jnp.cos(phases), jnp.sin(phases))


def rotate(field, cosine_rows, sine_rows):
    half_rot = ROT // 2
    first_half = field[:, :, :half_rot]
    second_half = field[:, :, half_rot:ROT]
    cos_rows = cosine_rows[:, None, :]
    sin_rows = sine_rows[:, None, :]
    return jnp.concatenate(
        [
            first_half * cos_rows - second_half * sin_rows,
            second_half * cos_rows + first_half * sin_rows,
            field[:, :, ROT:],
        ],
        axis=2,
    )


def rotate_back(field, cosine_rows, sine_rows):
    half_rot = ROT // 2
    first_half = field[:, :, :half_rot]
    second_half = field[:, :, half_rot:ROT]
    cos_rows = cosine_rows[:, None, :]
    sin_rows = sine_rows[:, None, :]
    return jnp.concatenate(
        [
            first_half * cos_rows + second_half * sin_rows,
            second_half * cos_rows - first_half * sin_rows,
            field[:, :, ROT:],
        ],
        axis=2,
    )


def contract_rows(left_side, right_side):
    return lax.dot_general(
        left_side, right_side, (((0,), (0,)), ((), ())), preferred_element_type=jnp.float32
    )


def contract_cols(left_side, right_side):
    return lax.dot_general(
        left_side, right_side, (((1,), (1,)), ((), ())), preferred_element_type=jnp.float32
    )


def gelu_back(hidden, act_grad):
    unused, pullback = jax.vjp(partial(jax.nn.gelu, approximate=False), hidden)
    return pullback(act_grad)[0]


def piece_mask(lengths, query_seg, query_index, first_index, row_count):
    key_seg, key_index, unused = locate(lengths, first_index, row_count)
    return (
        (key_seg[None, :] == query_seg[:, None])
        & (key_index[None, :] <= query_index[:, None])
        & (key_index[None, :] >= 0)
    )


def piece_scores(queries, key_block, allowed):
    scores = jnp.einsum(
        "qhd,khd->hqk", queries, key_block, preferred_element_type=jnp.float32
    ) * HEAD ** (-0.5)
    return jnp.where(allowed[None], scores, masked_score)


def adam_update(
    weight, first_moment, second_moment, grad_value, step_rate, decay_coef, first_fix, second_fix
):
    new_first = beta_first * first_moment + (1.0 - beta_first) * grad_value
    new_second = beta_second * second_moment + (1.0 - beta_second) * grad_value * grad_value
    step_ratio = new_first / first_fix / (jnp.sqrt(new_second / second_fix) + adam_eps)
    return (weight - step_rate * (step_ratio + decay_coef * weight), new_first, new_second)


def shards(
    tokens,
    cotangent,
    seq_lengths,
    step_count,
    norm_params,
    norm_first,
    norm_second,
    proj_weight,
    proj_first,
    proj_second,
    merge_weight,
    merge_first,
    merge_second,
    up_weight,
    up_first,
    up_second,
    down_weight,
    down_first,
    down_second,
):
    tok_rows = tokens.shape[0]
    narrow_count = lax.axis_size("narrow")
    wide_count = lax.axis_size("wide")
    span_index = lax.axis_index("narrow")
    group_rows = tok_rows * narrow_count
    longest = min(SEQ_MOST, group_rows * 3 // 4)
    reach_back = (longest + tok_rows - 2) // tok_rows
    lengths = seq_lengths[0]
    score_scale = HEAD ** (-0.5)
    proj_part = proj_weight.astype(jnp.bfloat16)
    merge_part = merge_weight.astype(jnp.bfloat16)
    proj_rows, merge_rows = (
        lax.all_gather(proj_part, "wide", axis=1, tiled=True),
        lax.all_gather(merge_part, "wide", axis=1, tiled=True),
    )
    proj_copy, merge_copy = (
        lax.all_gather(proj_rows, "narrow", axis=0, tiled=True),
        lax.all_gather(merge_rows, "narrow", axis=0, tiled=True),
    )
    up_slice = up_weight.astype(jnp.bfloat16)
    down_slice = down_weight.astype(jnp.bfloat16)
    residual = tokens.astype(jnp.float32)
    center = residual - jnp.mean(residual, axis=1, keepdims=True)
    inv_std = lax.rsqrt(jnp.mean(center * center, axis=1, keepdims=True) + norm_eps)
    unit_rows = center * inv_std
    normed = (unit_rows * norm_params[0] + norm_params[1]).astype(jnp.bfloat16)
    projected = jnp.dot(normed, proj_copy, preferred_element_type=jnp.float32)
    first_row = span_index * tok_rows
    query_seg, query_index, query_pos = locate(lengths, first_row, tok_rows)
    cosine_rows, sine_rows = rotary_tables(query_pos)
    queries = rotate(
        projected[:, :D].reshape(tok_rows, HEADS, HEAD), cosine_rows, sine_rows
    ).astype(jnp.bfloat16)
    own_keys = rotate(
        projected[:, D : 2 * D].reshape(tok_rows, HEADS, HEAD), cosine_rows, sine_rows
    ).astype(jnp.bfloat16)
    own_values = projected[:, 2 * D :].astype(jnp.bfloat16)
    own_pack = jnp.concatenate([own_keys.reshape(tok_rows, D), own_values], axis=1)

    def unpack(key_pack):
        return (
            key_pack[:, :D].reshape(tok_rows, HEADS, HEAD),
            key_pack[:, D:].reshape(tok_rows, HEADS, HEAD),
        )

    key_packs = [own_pack]
    run_max = None
    run_sum = None
    weighted = None
    for distance in range(reach_back + 1):
        if distance == 0:
            key_pack = own_pack
        else:
            key_pack = from_behind(own_pack, "narrow", distance)
            key_packs.append(key_pack)
        allowed = piece_mask(
            lengths, query_seg, query_index, first_row - distance * tok_rows, tok_rows
        )
        key_block, value_block = unpack(key_pack)
        scores = piece_scores(queries, key_block, allowed)
        piece_max = jnp.max(scores, axis=2)
        if distance == 0:
            new_max = piece_max
            weights = jnp.exp(scores - new_max[:, :, None])
            run_sum = jnp.sum(weights, axis=2)
            weighted = jnp.einsum(
                "hqk,khd->hqd",
                weights.astype(jnp.bfloat16),
                value_block,
                preferred_element_type=jnp.float32,
            )
        else:
            new_max = jnp.maximum(run_max, piece_max)
            factor = jnp.exp(run_max - new_max)
            weights = jnp.exp(scores - new_max[:, :, None])
            run_sum = run_sum * factor + jnp.sum(weights, axis=2)
            weighted = weighted * factor[:, :, None] + jnp.einsum(
                "hqk,khd->hqd",
                weights.astype(jnp.bfloat16),
                value_block,
                preferred_element_type=jnp.float32,
            )
        run_max = new_max
    log_total = run_max + jnp.log(run_sum)
    attended_heads = weighted / run_sum[:, :, None]
    attended = jnp.transpose(attended_heads, (1, 0, 2)).reshape(tok_rows, D).astype(jnp.bfloat16)
    merged = jnp.dot(attended, merge_copy, preferred_element_type=jnp.float32)
    gathered = lax.all_gather(normed, "narrow", axis=0, tiled=True)
    hidden = jnp.dot(gathered, up_slice, preferred_element_type=jnp.float32)
    activated = jax.nn.gelu(hidden, approximate=False).astype(jnp.bfloat16)
    rows_part = activated
    branch = lax.psum_scatter(
        jnp.dot(rows_part, down_slice, preferred_element_type=jnp.float32).astype(jnp.bfloat16),
        "narrow",
        scatter_dimension=0,
        tiled=True,
    ).astype(jnp.float32)
    output_rows = residual + merged + branch
    layer_out = output_rows.astype(jnp.bfloat16)
    grad_rows = cotangent.astype(jnp.float32)
    grads_all = lax.all_gather(cotangent, "narrow", axis=0, tiled=True)
    down_grad = contract_rows(activated, grads_all)
    act_grad = contract_cols(grads_all, down_slice)
    hidden_grad = gelu_back(hidden, act_grad).astype(jnp.bfloat16)
    up_grad = contract_rows(gathered, hidden_grad)
    rows_part = hidden_grad
    branch_back = lax.psum_scatter(
        contract_cols(rows_part, up_slice).astype(jnp.bfloat16),
        "narrow",
        scatter_dimension=0,
        tiled=True,
    ).astype(jnp.float32)
    up_sum, down_sum = (
        lax.psum(up_grad.astype(jnp.bfloat16), "wide").astype(jnp.float32),
        lax.psum(down_grad.astype(jnp.bfloat16), "wide").astype(jnp.float32),
    )
    merge_grad = contract_rows(attended, cotangent)
    attended_grad = (
        contract_cols(cotangent, merge_copy).astype(jnp.bfloat16).reshape(tok_rows, HEADS, HEAD)
    )
    row_delta = jnp.einsum(
        "qhd,hqd->hq", attended_grad, attended_heads, preferred_element_type=jnp.float32
    )
    query_grad = jnp.zeros((tok_rows, HEADS, HEAD), jnp.float32)
    pack_grad = None
    for distance in range(reach_back + 1):
        if distance == 0:
            key_pack = own_pack
        else:
            key_pack = key_packs[distance]
        allowed = piece_mask(
            lengths, query_seg, query_index, first_row - distance * tok_rows, tok_rows
        )
        key_block, value_block = unpack(key_pack)
        scores = piece_scores(queries, key_block, allowed)
        prob_rows = jnp.exp(scores - log_total[:, :, None])
        value_grad = jnp.einsum(
            "hqk,qhd->khd",
            prob_rows.astype(jnp.bfloat16),
            attended_grad,
            preferred_element_type=jnp.float32,
        )
        prob_grad = jnp.einsum(
            "qhd,khd->hqk", attended_grad, value_block, preferred_element_type=jnp.float32
        )
        score_grad = (prob_rows * (prob_grad - row_delta[:, :, None])).astype(jnp.bfloat16)
        query_grad = (
            query_grad
            + jnp.einsum("hqk,khd->qhd", score_grad, key_block, preferred_element_type=jnp.float32)
            * score_scale
        )
        key_grad = (
            jnp.einsum("hqk,qhd->khd", score_grad, queries, preferred_element_type=jnp.float32)
            * score_scale
        )
        grad_pack = jnp.concatenate(
            [key_grad.reshape(tok_rows, D), value_grad.reshape(tok_rows, D)], axis=1
        )
        if distance == 0:
            pack_grad = grad_pack
        else:
            pack_grad = pack_grad + from_behind(
                grad_pack.astype(jnp.bfloat16), "narrow", -distance
            ).astype(grad_pack.dtype)
    key_total = rotate_back(pack_grad[:, :D].reshape(tok_rows, HEADS, HEAD), cosine_rows, sine_rows)
    query_total = rotate_back(query_grad, cosine_rows, sine_rows)
    mixed_grad = jnp.concatenate(
        [query_total.reshape(tok_rows, D), key_total.reshape(tok_rows, D), pack_grad[:, D:]], axis=1
    ).astype(jnp.bfloat16)
    proj_grad = contract_rows(normed, mixed_grad)
    normed_grad = contract_cols(mixed_grad, proj_copy) + branch_back
    gain_grad = jnp.sum(normed_grad * unit_rows, axis=0)
    bias_grad = jnp.sum(normed_grad, axis=0)
    unit_grad = normed_grad * norm_params[0]
    input_grad = grad_rows + inv_std * (
        unit_grad
        - jnp.mean(unit_grad, axis=1, keepdims=True)
        - unit_rows * jnp.mean(unit_grad * unit_rows, axis=1, keepdims=True)
    )
    proj_within, merge_within = (
        lax.psum_scatter(
            proj_grad.astype(jnp.bfloat16), "narrow", scatter_dimension=0, tiled=True
        ).astype(jnp.float32),
        lax.psum_scatter(
            merge_grad.astype(jnp.bfloat16), "narrow", scatter_dimension=0, tiled=True
        ).astype(jnp.float32),
    )
    proj_block, merge_block = (
        lax.psum_scatter(
            proj_within.astype(jnp.bfloat16), "wide", scatter_dimension=1, tiled=True
        ).astype(jnp.float32),
        lax.psum_scatter(
            merge_within.astype(jnp.bfloat16), "wide", scatter_dimension=1, tiled=True
        ).astype(jnp.float32),
    )
    local_squares = (
        jnp.sum(proj_block * proj_block)
        + jnp.sum(merge_block * merge_block)
        + (jnp.sum(up_sum * up_sum) + jnp.sum(down_sum * down_sum)) / wide_count
    )
    norm_part = jnp.stack([gain_grad, bias_grad])
    branch_part = jnp.stack([jnp.sum(merged * merged), jnp.sum(branch * branch)])
    square_total, norm_total, output_squares, branch_squares = lax.psum(
        (
            local_squares.reshape(1),
            norm_part,
            jnp.sum(output_rows * output_rows).reshape(1),
            branch_part,
        ),
        ("wide", "narrow"),
    )
    grad_norm = jnp.sqrt(square_total + jnp.sum(norm_total * norm_total))
    clip_factor = jnp.minimum(1.0, math.sqrt(NPARAMS) / grad_norm)
    entry_count = wide_count * group_rows * D
    residual_rms = jnp.sqrt(output_squares / entry_count)
    branch_norms = jnp.sqrt(branch_squares / entry_count)
    step_value = step_count[0].astype(jnp.float32)
    first_fix = 1.0 - jnp.power(beta_first, step_value)
    second_fix = 1.0 - jnp.power(beta_second, step_value)
    ramp = jnp.minimum(1.0, step_value / warmup_steps)
    norm_clipped = norm_total * clip_factor
    new_norm = adam_update(
        norm_params,
        norm_first,
        norm_second,
        norm_clipped,
        norm_rate * ramp,
        0.0,
        first_fix,
        second_fix,
    )
    new_proj = adam_update(
        proj_weight,
        proj_first,
        proj_second,
        proj_block * clip_factor,
        matrix_rate * ramp,
        decay_rate,
        first_fix,
        second_fix,
    )
    new_merge = adam_update(
        merge_weight,
        merge_first,
        merge_second,
        merge_block * clip_factor,
        matrix_rate * ramp,
        decay_rate,
        first_fix,
        second_fix,
    )
    new_up = adam_update(
        up_weight,
        up_first,
        up_second,
        up_sum * clip_factor,
        matrix_rate * ramp,
        decay_rate,
        first_fix,
        second_fix,
    )
    new_down = adam_update(
        down_weight,
        down_first,
        down_second,
        down_sum * clip_factor,
        matrix_rate * ramp,
        decay_rate,
        first_fix,
        second_fix,
    )
    return (
        layer_out,
        input_grad,
        grad_norm,
        residual_rms,
        norm_clipped,
        new_norm[0],
        new_norm[1],
        new_norm[2],
        new_proj[0],
        new_proj[1],
        new_proj[2],
        new_merge[0],
        new_merge[1],
        new_merge[2],
        new_up[0],
        new_up[1],
        new_up[2],
        new_down[0],
        new_down[1],
        new_down[2],
        branch_norms,
        new_proj[0].astype(jnp.bfloat16),
        new_merge[0].astype(jnp.bfloat16),
        new_up[0].astype(jnp.bfloat16),
        new_down[0].astype(jnp.bfloat16),
    )


def solution(mesh):
    placed = (
        P(("wide", "narrow"), None),
        P(("wide", "narrow"), None),
        P("wide", None),
        P(),
        P(),
        P(),
        P(),
        P("narrow", "wide"),
        P("narrow", "wide"),
        P("narrow", "wide"),
        P("narrow", "wide"),
        P("narrow", "wide"),
        P("narrow", "wide"),
        P(None, "narrow"),
        P(None, "narrow"),
        P(None, "narrow"),
        P("narrow", None),
        P("narrow", None),
        P("narrow", None),
    )
    return jax.shard_map(
        shards,
        mesh=mesh,
        in_specs=placed,
        out_specs=(
            P(("wide", "narrow"), None),
            P(("wide", "narrow"), None),
            P(),
            P(),
            P(),
            P(),
            P(),
            P(),
            P("narrow", "wide"),
            P("narrow", "wide"),
            P("narrow", "wide"),
            P("narrow", "wide"),
            P("narrow", "wide"),
            P("narrow", "wide"),
            P(None, "narrow"),
            P(None, "narrow"),
            P(None, "narrow"),
            P("narrow", None),
            P("narrow", None),
            P("narrow", None),
            P(),
            P("narrow", "wide"),
            P("narrow", "wide"),
            P(None, "narrow"),
            P("narrow", None),
        ),
        check_vma=False,
    )
```

profile of v0, /device:TPU:0, one launch (start us, length us, event | category | flops | bytes accessed | tf_op | source)
XLA Modules:
  0.0 1426.5 jit_solution(14545300754538221926)
XLA Ops:
  10.0 12.5 all_gather.20
  22.6 16.4 %all-gather.6.cloned.1.call-done = bf16[256,3072]{1,0:T(8,128)(2,1)} async-done(((bf16[256,384]{1,0:T(8,128)(2,1)}), bf16[256,3072]{1,0:T(8,128)(2,1)}) %all-gather.6.cloned.1.call-update) | async-done | bytes 1572880 | tf_op jit(solution)/shard_map/all_gather | solution.py:160
  45.5 40.8 %all-gather.10.cloned.1.call-done = bf16[1024,1024]{1,0:T(8,128)(2,1)} async-done(((bf16[256,1024]{1,0:T(8,128)(2,1)}), bf16[1024,1024]{1,0:T(8,128)(2,1)}) %all-gather.10.cloned.1.call-update) | async-done | bytes 2097168 | tf_op jit(solution)/shard_map/all_gather | solution.py:165
  90.5 111.5 %all-gather.8.cloned.1.call-done = bf16[1024,3072]{1,0:T(8,128)(2,1)} async-done(((bf16[256,3072]{1,0:T(8,128)(2,1)}), bf16[1024,3072]{1,0:T(8,128)(2,1)}) %all-gather.8.cloned.1.call-update) | async-done | bytes 6291472 | tf_op jit(solution)/shard_map/all_gather | solution.py:164
  266.3 57.6 %collective-permute-done.2 = bf16[512,2048]{1,0:T(8,128)(2,1)} collective-permute-done((bf16[512,2048]{1,0:T(8,128)(2,1)}, bf16[512,2048]{1,0:T(8,128)(2,1)}, u32[]{:S(2)}, u32[]{:S(2)}) %collective-permute-start.2) | collective-permute-done | bytes 2097184 | tf_op jit(solution)/shard_map/ppermute | solution.py:31
  328.0 40.9 %collective-permute-done.1 = bf16[512,2048]{1,0:T(8,128)(2,1)} collective-permute-done((bf16[512,2048]{1,0:T(8,128)(2,1)}, bf16[512,2048]{1,0:T(8,128)(2,1)}, u32[]{:S(2)}, u32[]{:S(2)}) %collective-permute-start.1) | collective-permute-done | bytes 2097184 | tf_op jit(solution)/shard_map/ppermute | solution.py:31
  372.1 51.5 %collective-permute-done = bf16[512,2048]{1,0:T(8,128)(2,1)} collective-permute-done((bf16[512,2048]{1,0:T(8,128)(2,1)}, bf16[512,2048]{1,0:T(8,128)(2,1)}, u32[]{:S(2)}, u32[]{:S(2)}) %collective-permute-start) | collective-permute-done | bytes 2097184 | tf_op jit(solution)/shard_map/ppermute | solution.py:31
  483.5 9.9 fusion.23
  493.5 10.1 fusion.25
  514.4 26.6 %multiply_convert_fusion.4 = (bf16[2048,1024]{1,0:T(8,128)(2,1)}, f32[2048,1024]{1,0:T(8,128)}, f32[2048,1024]{1,0:T(8,128)}) fusion(bf16[2048,1024]{1,0:T(8,128)(2,1)} %all-gather.12.cloned.1.call-done, f32[1024,1024]{1,0:T(8,128)} %param.32), kind=kOutput, calls=%fused_computation.43 | convolution fusion | flops 4432330752 | bytes 29360128 | tf_op jit(solution)/shard_map/dot_general | solution.py:236
  550.5 11.5 add_convert_fusion
  613.8 12.1 multiply_convert_fusion.1
  625.9 12.2 multiply_convert_fusion
  714.8 173.7 %collective-permute-done.4 = bf16[512,2048]{0,1:T(8,128)(2,1)} collective-permute-done((bf16[512,2048]{0,1:T(8,128)(2,1)}, bf16[512,2048]{0,1:T(8,128)(2,1)}, u32[]{:S(2)}, u32[]{:S(2)}) %collective-permute-start.4) | collective-permute-done | bytes 2097184 | tf_op jit(solution)/shard_map/ppermute | solution.py:31
  888.5 46.1 %collective-permute-done.3 = bf16[512,2048]{0,1:T(8,128)(2,1)} collective-permute-done((bf16[512,2048]{0,1:T(8,128)(2,1)}, bf16[512,2048]{0,1:T(8,128)(2,1)}, u32[]{:S(2)}, u32[]{:S(2)}) %collective-permute-start.3) | collective-permute-done | bytes 2097184 | tf_op jit(solution)/shard_map/ppermute | solution.py:31
  952.1 10.0 convolution_convert_fusion.1
  962.6 10.0 convolution_convert_fusion.2
  980.8 123.1 %reduce-scatter.15.cloned.1.call-done = bf16[256,3072]{1,0:T(8,128)(2,1)} async-done(((bf16[1024,3072]{1,0:T(8,128)(2,1)}), bf16[256,3072]{1,0:T(8,128)(2,1)}) %reduce-scatter.15.cloned.1.call-update) | async-done | bytes 1572880 | tf_op jit(solution)/shard_map/reduce_scatter | solution.py:328
  1106.5 77.6 %reduce-scatter.13.cloned.1.call-done = bf16[512,1024]{1,0:T(8,128)(2,1)} async-done(((bf16[2048,1024]{1,0:T(8,128)(2,1)}), bf16[512,1024]{1,0:T(8,128)(2,1)}) %reduce-scatter.13.cloned.1.call-update) | async-done | bytes 1048592 | tf_op jit(solution)/shard_map/reduce_scatter | solution.py:254
  1191.5 72.6 %reduce-scatter.11.cloned.1.call-done = bf16[512,1024]{1,0:T(8,128)(2,1)} async-done(((bf16[2048,1024]{1,0:T(8,128)(2,1)}), bf16[512,1024]{1,0:T(8,128)(2,1)}) %reduce-scatter.11.cloned.1.call-update) | async-done | bytes 1048592 | tf_op jit(solution)/shard_map/reduce_scatter | solution.py:239
  1276.4 26.1 %reduce-scatter.21.cloned.1.call-done = bf16[128,256]{1,0:T(8,128)(2,1)} async-done(((bf16[1024,256]{1,0:T(8,128)(2,1)}), bf16[128,256]{1,0:T(8,128)(2,1)}) %reduce-scatter.21.cloned.1.call-update) | async-done | bytes 65552
  1304.1 40.5 %reduce-scatter.19.cloned.1.call-done = bf16[384,256]{1,0:T(8,128)(2,1)} async-done(((bf16[3072,256]{1,0:T(8,128)(2,1)}), bf16[384,256]{1,0:T(8,128)(2,1)}) %reduce-scatter.19.cloned.1.call-update) | async-done | bytes 196624
  1347.7 40.2 %all-reduce = (f32[1]{0:T(128)}, f32[2,1024]{1,0:T(2,128)S(1)}, f32[1]{0:T(128)}, f32[2]{0:T(128)S(1)}) all-reduce(f32[1]{0:T(128)} %bitcast.53, f32[2,1024]{1,0:T(2,128)S(1)} %pad_maximum_fusion.10, f32[1]{0:T(128)} %bitcast.57, f32[2]{0:T(128)} %pad_maximum_fusion.11), channel_id=1, replica_groups=mesh['wide'=8,'narrow'=4] {'wide','narrow'}, use_global_device_ids=true, to_apply=%region_30.31 | all-reduce | flops 2052 | bytes 16416 | tf_op jit(solution)/shard_map/psum | solution.py:350
  1396.7 11.1 fusion.99
  (359 shorter events, 358.1 us)
Async XLA Ops:
  7.2 31.8 %all-gather.6.cloned.1.call-start = ((), (), s32[]{:S(2)}) async-start(), calls=%async_computation.6 | async-start | bytes 1769472 | tf_op jit(solution)/shard_map/all_gather | solution.py:160
  9.1 77.2 %all-gather.10.cloned.1.call-start = ((), (), s32[]{:S(2)}) async-start(), calls=%async_computation.8 | async-start | bytes 2621440 | tf_op jit(solution)/shard_map/all_gather | solution.py:165
  22.6 179.5 %all-gather.8.cloned.1.call-start = ((), (), s32[]{:S(2)}) async-start(), calls=%async_computation.7 | async-start | bytes 7864320 | tf_op jit(solution)/shard_map/all_gather | solution.py:164
  39.0 475.3 %all-gather.12.cloned.1.call-start = ((), (), s32[]{:S(2)}) async-start(), calls=%async_computation.9 | async-start | bytes 5242880 | tf_op jit(solution)/shard_map/all_gather | solution.py:235
  41.8 499.2 %all-gather.14.cloned.1.call-start = ((), (), s32[]{:S(2)}) async-start(), calls=%async_computation.11 | async-start | bytes 5242880 | tf_op jit(solution)/shard_map/all_gather | solution.py:248
  42.4 930.3 %reduce-scatter.17.cloned.1.call-start = ((), (), s32[]{:S(2)}) async-start(), calls=%async_computation.14 | async-start | bytes 2621440 | tf_op jit(solution)/shard_map/reduce_scatter | solution.py:331
  43.1 175.7 %copy-start.67 = (f32[512,8]{0,1:T(8,128)}, f32[512,8]{0,1:T(8,128)S(1)}, u32[]{:S(2)}) copy-start(f32[512,8]{0,1:T(8,128)S(1)} %get-tuple-element.105) | copy-start | bytes 49156
  43.1 175.7 %copy-start.69 = (f32[512,8]{0,1:T(8,128)}, f32[512,8]{0,1:T(8,128)S(1)}, u32[]{:S(2)}) copy-start(f32[512,8]{0,1:T(8,128)S(1)} %get-tuple-element.106) | copy-start | bytes 49156
  214.5 229.9 %copy-start.1 = (bf16[512,16,48]{0,2,1:T(8,128)(2,1)}, bf16[512,16,48]{0,2,1:T(8,128)(2,1)S(1)}, u32[]{:S(2)}) copy-start(bf16[512,16,48]{0,2,1:T(8,128)(2,1)S(1)} %slice.160) | copy-start | bytes 2359300
  218.8 225.6 %copy-start.34 = (bf16[512,16,8]{0,2,1:T(8,128)(2,1)}, bf16[512,16,8]{0,2,1:T(8,128)(2,1)S(1)}, u32[]{:S(2)}) copy-start(bf16[512,16,8]{0,2,1:T(8,128)(2,1)S(1)} %get-tuple-element.87) | copy-start | bytes 393220
  218.8 225.6 %copy-start.36 = (bf16[512,16,8]{0,2,1:T(8,128)(2,1)}, bf16[512,16,8]{0,2,1:T(8,128)(2,1)S(1)}, u32[]{:S(2)}) copy-start(bf16[512,16,8]{0,2,1:T(8,128)(2,1)S(1)} %get-tuple-element.88) | copy-start | bytes 393220
  230.8 93.1 %collective-permute-start.2 = (bf16[512,2048]{1,0:T(8,128)(2,1)}, bf16[512,2048]{1,0:T(8,128)(2,1)}, u32[]{:S(2)}, u32[]{:S(2)}) collective-permute-start(bf16[512,2048]{1,0:T(8,128)(2,1)} %pad_maximum_fusion.1), channel_id=1, source_target_pairs={{0,3},{4,7},{8,11},{12,15},{16,19},{20,23},{24,27},{28,31}} | collective-permute-start | bytes 6291464 | tf_op jit(solution)/shard_map/ppermute | solution.py:31
  234.6 134.3 %collective-permute-start.1 = (bf16[512,2048]{1,0:T(8,128)(2,1)}, bf16[512,2048]{1,0:T(8,128)(2,1)}, u32[]{:S(2)}, u32[]{:S(2)}) collective-permute-start(bf16[512,2048]{1,0:T(8,128)(2,1)} %pad_maximum_fusion.1), channel_id=1, source_target_pairs={{0,2},{1,3},{4,6},{5,7},{8,10},{9,11},{12,14},{13,15},{16,18},{17,... | collective-permute-start | bytes 6291464 | tf_op jit(solution)/shard_map/ppermute | solution.py:31
  237.2 186.4 %collective-permute-start = (bf16[512,2048]{1,0:T(8,128)(2,1)}, bf16[512,2048]{1,0:T(8,128)(2,1)}, u32[]{:S(2)}, u32[]{:S(2)}) collective-permute-start(bf16[512,2048]{1,0:T(8,128)(2,1)} %pad_maximum_fusion.1), channel_id=1, source_target_pairs={{0,1},{1,2},{2,3},{4,5},{5,6},{6,7},{8,9},{9,10},{10,11},{12,13},{... | collective-permute-start | bytes 6291464 | tf_op jit(solution)/shard_map/ppermute | solution.py:31
  514.3 461.2 %all-reduce.4.cloned.1.call-start = ((), (), s32[]{:S(2)}) async-start(), calls=%async_computation.17 | async-start | bytes 8388608 | tf_op jit(solution)/shard_map/psum | solution.py:261
  569.9 533.9 %reduce-scatter.15.cloned.1.call-start = ((), (), s32[]{:S(2)}) async-start(), calls=%async_computation.13 | async-start | bytes 7864320 | tf_op jit(solution)/shard_map/reduce_scatter | solution.py:328
  687.1 201.4 %collective-permute-start.4 = (bf16[512,2048]{0,1:T(8,128)(2,1)}, bf16[512,2048]{0,1:T(8,128)(2,1)}, u32[]{:S(2)}, u32[]{:S(2)}) collective-permute-start(bf16[512,2048]{0,1:T(8,128)(2,1)} %pad_maximum_fusion.3), channel_id=1, source_target_pairs={{2,0},{3,1},{6,4},{7,5},{10,8},{11,9},{14,12},{15,13},{18,16},{19,... | collective-permute-start | bytes 6291464 | tf_op jit(solution)/shard_map/ppermute | solution.py:31
  691.6 242.9 %collective-permute-start.3 = (bf16[512,2048]{0,1:T(8,128)(2,1)}, bf16[512,2048]{0,1:T(8,128)(2,1)}, u32[]{:S(2)}, u32[]{:S(2)}) collective-permute-start(bf16[512,2048]{0,1:T(8,128)(2,1)} %pad_maximum_fusion.2), channel_id=1, source_target_pairs={{1,0},{2,1},{3,2},{5,4},{6,5},{7,6},{9,8},{10,9},{11,10},{13,12},{... | collective-permute-start | bytes 6291464 | tf_op jit(solution)/shard_map/ppermute | solution.py:31
  695.7 238.8 %collective-permute-start.5 = (bf16[512,2048]{0,1:T(8,128)(2,1)}, bf16[512,2048]{0,1:T(8,128)(2,1)}, u32[]{:S(2)}, u32[]{:S(2)}) collective-permute-start(bf16[512,2048]{0,1:T(8,128)(2,1)} %pad_maximum_fusion.4), channel_id=1, source_target_pairs={{3,0},{7,4},{11,8},{15,12},{19,16},{23,20},{27,24},{31,28}} | collective-permute-start | bytes 6291464 | tf_op jit(solution)/shard_map/ppermute | solution.py:31
  952.0 232.0 %reduce-scatter.13.cloned.1.call-start = ((), (), s32[]{:S(2)}) async-start(), calls=%async_computation.12 | async-start | bytes 5242880 | tf_op jit(solution)/shard_map/reduce_scatter | solution.py:254
  962.2 302.0 %reduce-scatter.11.cloned.1.call-start = ((), (), s32[]{:S(2)}) async-start(), calls=%async_computation.10 | async-start | bytes 5242880 | tf_op jit(solution)/shard_map/reduce_scatter | solution.py:239
  972.6 329.8 %reduce-scatter.21.cloned.1.call-start = ((), (), s32[]{:S(2)}) async-start(), calls=%async_computation.16 | async-start | bytes 589824
  974.8 369.8 %reduce-scatter.19.cloned.1.call-start = ((), (), s32[]{:S(2)}) async-start(), calls=%async_computation.15 | async-start | bytes 1769472
  1106.5 157.7 %copy-start.4 = (bf16[512,1024]{1,0:T(8,128)(2,1)S(1)}, bf16[512,1024]{1,0:T(8,128)(2,1)}, u32[]{:S(2)}) copy-start(bf16[512,1024]{1,0:T(8,128)(2,1)} %param.19) | copy-start | bytes 3145732
  (100 other events, 2073.7 us)
Sparse Core Ops, SparseCore 0:
  10.5 28.4 all-gather.5
  40.6 45.6 all-gather.9
  87.9 114.1 all-gather.7
  204.0 119.4 all-gather.11
  325.0 156.4 all-gather.13
  514.4 146.8 reduce-scatter.16
  664.7 89.6 all-reduce.3
  952.2 151.6 reduce-scatter.14
  1106.7 77.2 reduce-scatter.12
  1186.8 77.2 reduce-scatter.10
  1267.8 34.6 reduce-scatter.20
  1306.2 38.3 reduce-scatter.18
where the time goes:
time: 1430 us
  waiting for transfers between devices  879 us (61%)
  matrix products  299 us (21%)
  other arithmetic  108 us (8%)
  blocking collectives  52.7 us (4%)
  local copies, waits for them, and re-layouts  50 us (3%)
  between operations  23.4 us (2%)
  starting transfers between devices  14.3 us (1%)
    ppermute x6, waiting for transfers between devices, from_behind(): return lax.ppermute(array, axis, pairs)  370 us
    reduce_scatter x1, waiting for transfers between devices, shards(): lax.psum_scatter(proj_grad.astype(jnp.bfloat16), 'narrow', scatter_dimens...  123 us
    all_gather x1, waiting for transfers between devices, shards(): lax.all_gather(proj_rows, 'narrow', axis=0, tiled=True)  112 us
    reduce_scatter x1, waiting for transfers between devices, shards(): lax.psum_scatter(contract_cols(rows_part, up_slice).astype(jnp.bfloat16),...  77.6 us
    reduce_scatter x1, waiting for transfers between devices, shards(): lax.psum_scatter(jnp.dot(rows_part, down_slice, preferred_element_type=jn...  72.6 us
    unnamed x14, waiting for transfers between devices  67.3 us
    all_gather x1, waiting for transfers between devices, shards(): lax.all_gather(merge_rows, 'narrow', axis=0, tiled=True)  40.8 us
    psum x1, blocking collectives, shards(): lax.psum((local_squares.reshape(1), norm_part, jnp.sum(output_rows * outp...  40.2 us
  transfers between devices with their start and end apart: 18, of which 13 were waited for; matrix products, arithmetic and copies ran while one was open for 30% of the time, Pallas kernels for 0%

commit v1 on v0

v1 whole, which is shorter than its diff:
```python
from functools import partial
import math

import jax
import jax.numpy as jnp
from jax import lax
from jax.experimental import pallas as pl
from jax.experimental.pallas import tpu as pltpu
from jax.sharding import PartitionSpec as P

HEADS = 16
HEAD = 64
D = 1024
ROT = 16
LANES = 128
ROW_BLOCK = 512
NPARAMS = 12584960


norm_eps = 1e-05
adam_eps = 1e-08
beta_first = 0.5
beta_second = 0.5
decay_rate = 0.01
matrix_rate = 0.1
norm_rate = 1.0
warmup_steps = 20.0
masked_score = -1e30


def dot_last(left_side, right_side):
    return lax.dot_general(
        left_side, right_side, (((1,), (1,)), ((), ())), preferred_element_type=jnp.float32
    )


def dot_plain(left_side, right_side):
    return lax.dot_general(
        left_side, right_side, (((1,), (0,)), ((), ())), preferred_element_type=jnp.float32
    )


def dot_first(left_side, right_side):
    return lax.dot_general(
        left_side, right_side, (((0,), (0,)), ((), ())), preferred_element_type=jnp.float32
    )


def locate(lengths, token_index):
    seq_ends = jnp.cumsum(lengths)
    starts = seq_ends - lengths
    segment = jnp.sum(
        (seq_ends[None, :] <= token_index[:, None]).astype(jnp.int32), axis=1, dtype=jnp.int32
    )
    choose = segment[:, None] == jnp.arange(lengths.shape[0], dtype=jnp.int32)[None, :]
    seq_start = jnp.sum(jnp.where(choose, starts[None, :], 0), axis=1, dtype=jnp.int32)
    seq_end = jnp.sum(jnp.where(choose, seq_ends[None, :], 0), axis=1, dtype=jnp.int32)
    return (seq_start, seq_end)


def rotary_tables(position):
    half_rot = ROT // 2
    frequency = jnp.power(10000.0, -2.0 * jnp.arange(half_rot, dtype=jnp.float32) / ROT)
    row = jnp.concatenate([frequency, frequency, jnp.zeros((HEAD - ROT,), jnp.float32)])
    row = jnp.tile(row, LANES // HEAD)
    sign = jnp.where(jnp.arange(LANES) % HEAD < half_rot, -1.0, 1.0)
    phases = position.astype(jnp.float32)[:, None] * row[None, :]
    return (jnp.cos(phases), jnp.sin(phases) * sign[None, :])


def partner(field):
    half_rot = ROT // 2
    lane = lax.broadcasted_iota(jnp.int32, field.shape, 1) % HEAD
    return jnp.where(
        lane < half_rot,
        pltpu.roll(field, LANES - half_rot, 1),
        pltpu.roll(field, half_rot, 1),
    )


def project_kernel(rows_ref, weight_ref, cos_ref, sin_ref, out_ref):
    width = out_ref.shape[1]
    projected = dot_plain(rows_ref[...], weight_ref[...])
    for first in range(0, width, LANES):
        piece = projected[:, first : first + LANES]
        part = first // LANES % 3
        if part < 2:
            piece = piece * cos_ref[...] + partner(piece) * sin_ref[...]
        if part == 0:
            piece = piece * HEAD ** (-0.5)
        out_ref[:, first : first + LANES] = piece.astype(jnp.bfloat16)


def project(rows, weight, cosine, sine):
    count, depth = rows.shape
    width = weight.shape[1]
    block = min(ROW_BLOCK, count)
    return pl.pallas_call(
        project_kernel,
        out_shape=jax.ShapeDtypeStruct((count, width), jnp.bfloat16),
        grid=(count // block,),
        in_specs=[
            pl.BlockSpec((block, depth), lambda i: (i, 0)),
            pl.BlockSpec((depth, width), lambda i: (0, 0)),
            pl.BlockSpec((block, LANES), lambda i: (i, 0)),
            pl.BlockSpec((block, LANES), lambda i: (i, 0)),
        ],
        out_specs=pl.BlockSpec((block, width), lambda i: (i, 0)),
        cost_estimate=pl.CostEstimate(
            flops=2 * count * depth * width,
            bytes_accessed=2 * (count * depth + depth * width + count * width),
            transcendentals=0,
        ),
        name="project",
    )(rows, weight, cosine, sine)


def normalize(tokens):
    residual = tokens.astype(jnp.float32)
    center = residual - jnp.mean(residual, axis=1, keepdims=True)
    inv_std = lax.rsqrt(jnp.mean(center * center, axis=1, keepdims=True) + norm_eps)
    return (center * inv_std, inv_std)


def feed_kernel(tokens_ref, params_ref, weight_ref, *refs):
    normed_ref, act_ref, slope_ref = refs[-3:]
    unit, unused = normalize(tokens_ref[...])
    normed_ref[...] = (unit * params_ref[0:1, :] + params_ref[1:2, :]).astype(jnp.bfloat16)
    width = act_ref.shape[1]
    step = min(256, width)
    for first in range(0, width, step):
        hidden = dot_plain(normed_ref[...], weight_ref[:, first : first + step])
        share = 0.5 + 0.5 * lax.erf(hidden * math.sqrt(0.5))
        bell = jnp.exp(hidden * hidden * -0.5) * (1.0 / math.sqrt(2.0 * math.pi))
        act_ref[:, first : first + step] = (hidden * share).astype(jnp.bfloat16)
        slope_ref[:, first : first + step] = share + hidden * bell


def feed(slot, slots, tokens, params, weight, held):
    rows, depth = tokens.shape
    width = weight.shape[1]
    whole = pl.BlockSpec(memory_space=pl.ANY)
    return pl.pallas_call(
        feed_kernel,
        out_shape=(
            jax.ShapeDtypeStruct((slots * rows, depth), jnp.bfloat16),
            jax.ShapeDtypeStruct((slots * rows, width), jnp.bfloat16),
            jax.ShapeDtypeStruct((slots * rows, width), jnp.float32),
        ),
        grid=(2,),
        in_specs=[
            pl.BlockSpec((rows // 2, depth), lambda i: (i, 0)),
            pl.BlockSpec((2, depth), lambda i: (0, 0)),
            pl.BlockSpec((depth, width), lambda i: (0, 0)),
        ]
        + [whole] * len(held),
        out_specs=(
            pl.BlockSpec((rows // 2, depth), lambda i: (2 * slot + i, 0)),
            pl.BlockSpec((rows // 2, width), lambda i: (2 * slot + i, 0)),
            pl.BlockSpec((rows // 2, width), lambda i: (2 * slot + i, 0)),
        ),
        input_output_aliases={3 + k: k for k in range(len(held))},
        cost_estimate=pl.CostEstimate(
            flops=2 * rows * depth * width,
            bytes_accessed=4 * rows * depth + 2 * depth * width + 6 * rows * width,
            transcendentals=2 * rows * width,
        ),
        name="feed",
    )(tokens, params, weight, *held)


def pull_kernel(mixed_ref, hidden_ref, proj_ref, up_ref, tokens_ref, out_ref, sums_ref):
    partial_grad = dot_last(mixed_ref[...], proj_ref[...]) + dot_last(hidden_ref[...], up_ref[...])
    out_ref[...] = partial_grad
    unit, unused = normalize(tokens_ref[...])
    gain = jnp.sum(partial_grad * unit, axis=0, keepdims=True)
    bias = jnp.sum(partial_grad, axis=0, keepdims=True)
    both = jnp.concatenate([gain, bias], axis=0)

    @pl.when(pl.program_id(0) == 0)
    def _():
        sums_ref[...] = both

    @pl.when(pl.program_id(0) > 0)
    def _():
        sums_ref[...] += both


def pull(slot, mixed, hidden_grad, proj, up, tokens):
    rows, depth = tokens.shape
    half = rows // 2
    return pl.pallas_call(
        pull_kernel,
        out_shape=(
            jax.ShapeDtypeStruct((rows, depth), jnp.float32),
            jax.ShapeDtypeStruct((2, depth), jnp.float32),
        ),
        grid=(2,),
        in_specs=[
            pl.BlockSpec((half, mixed.shape[1]), lambda i: (2 * slot + i, 0)),
            pl.BlockSpec((half, hidden_grad.shape[1]), lambda i: (2 * slot + i, 0)),
            pl.BlockSpec(proj.shape, lambda i: (0, 0)),
            pl.BlockSpec(up.shape, lambda i: (0, 0)),
            pl.BlockSpec((half, depth), lambda i: (i, 0)),
        ],
        out_specs=(
            pl.BlockSpec((half, depth), lambda i: (i, 0)),
            pl.BlockSpec((2, depth), lambda i: (0, 0)),
        ),
        cost_estimate=pl.CostEstimate(
            flops=2 * rows * depth * (mixed.shape[1] + hidden_grad.shape[1]),
            bytes_accessed=8 * rows * depth + 2 * depth * (proj.shape[1] + up.shape[1]),
            transcendentals=0,
        ),
        name="pull",
    )(mixed, hidden_grad, proj, up, tokens)


def pick_kernel(index_ref, all_ref, out_ref):
    out_ref[...] = all_ref[...].reshape(out_ref.shape)


def pick_proj(weight_all, span_index, own_width):
    narrow_count, shards, rows, cols = weight_all.shape
    units = own_width // LANES
    per_shard = cols // LANES - 1
    per_part = D // LANES

    def source(c, index_ref):
        unit = (c % 3) * per_part + index_ref[0] * units + c // 3
        return (0, unit // per_shard, 0, unit % per_shard)

    return pl.pallas_call(
        pick_kernel,
        out_shape=jax.ShapeDtypeStruct((D, 3 * own_width), jnp.bfloat16),
        grid_spec=pltpu.PrefetchScalarGridSpec(
            num_scalar_prefetch=1,
            grid=(3 * units,),
            in_specs=[pl.BlockSpec((narrow_count, 1, rows, LANES), source)],
            out_specs=pl.BlockSpec((D, LANES), lambda c, index_ref: (0, c)),
        ),
        cost_estimate=pl.CostEstimate(
            flops=0, bytes_accessed=12 * D * own_width, transcendentals=0
        ),
        name="pick_proj",
    )(span_index.reshape(1), weight_all)


def turn_kernel(slots_ref, all_ref, out_ref):
    narrow_count, unused, rows, cols = all_ref.shape
    for t in range(narrow_count):
        out_ref[t * rows : (t + 1) * rows, :] = all_ref[slots_ref[t], 0]


def pick_merge(weight_all, slots, own_width):
    narrow_count, shards, rows, cols = weight_all.shape
    return pl.pallas_call(
        turn_kernel,
        out_shape=jax.ShapeDtypeStruct((D, D), jnp.bfloat16),
        grid_spec=pltpu.PrefetchScalarGridSpec(
            num_scalar_prefetch=1,
            grid=(shards,),
            in_specs=[
                pl.BlockSpec(
                    (narrow_count, 1, rows, LANES),
                    lambda j, slots_ref: (0, j, 0, cols // LANES - 1),
                )
            ],
            out_specs=pl.BlockSpec((D, LANES), lambda j, slots_ref: (0, j)),
        ),
        cost_estimate=pl.CostEstimate(flops=0, bytes_accessed=4 * D * D, transcendentals=0),
        name="pick_merge",
    )(slots, weight_all)


def head_lanes(field, head):
    lane = lax.broadcasted_iota(jnp.int32, field.shape, 1)
    keep = (lane >= head * HEAD) & (lane < (head + 1) * HEAD)
    return jnp.where(keep, field, jnp.zeros_like(field))


def pair_allowed(start_row, key_first, key_count, query_first, query_count):
    key_index = key_first + lax.broadcasted_iota(jnp.int32, (key_count, query_count), 0)
    query_index = query_first + lax.broadcasted_iota(jnp.int32, (key_count, query_count), 1)
    return (key_index >= start_row) & (key_index <= query_index)


def attend_kernel(
    block_q,
    block_k,
    heads_in,
    slots_ref,
    first_ref,
    last_ref,
    start_ref,
    query_ref,
    key_ref,
    value_ref,
    *refs,
):
    out_ref, tall_ref, log_ref, turned, best, total, summed = refs[-7:]
    index = pl.program_id(0)
    key_blocks = key_ref.shape[0] // block_k

    @pl.when(index == 0)
    def _():
        for j in range(key_blocks):
            piece = value_ref[j * block_k : (j + 1) * block_k, :].astype(jnp.float32)
            turned[:, j * block_k : (j + 1) * block_k] = piece.T.astype(jnp.bfloat16)

    query_first = index * block_q
    low = first_ref[index] // block_k
    high = (query_first + block_q - 1) // block_k + 1
    start_row = start_ref[...]
    queries = [head_lanes(query_ref[...], head) for head in range(heads_in)]
    best[...] = jnp.full_like(best, masked_score)
    total[...] = jnp.zeros_like(total)
    summed[...] = jnp.zeros_like(summed)

    def visit(j, masked):
        key_rows = pl.ds(pl.multiple_of(slots_ref[j] * block_k, block_k), block_k)
        keys = key_ref[key_rows, :]
        if masked:
            allowed = pair_allowed(start_row, j * block_k, block_k, query_first, block_q)
        for head in range(heads_in):
            scores = dot_last(keys, queries[head])
            if masked:
                scores = jnp.where(allowed, scores, masked_score)
            old = best[head : head + 1, :]
            new = jnp.maximum(old, jnp.max(scores, axis=0, keepdims=True))
            weights = jnp.exp(scores - new)
            if masked:
                weights = jnp.where(allowed, weights, 0.0)
            factor = jnp.exp(old - new)
            best[head : head + 1, :] = new
            total[head : head + 1, :] = total[head : head + 1, :] * factor + jnp.sum(
                weights, axis=0, keepdims=True
            )
            rows = slice(head * HEAD, (head + 1) * HEAD)
            summed[rows, :] = summed[rows, :] * factor + dot_plain(
                turned[rows, key_rows], weights.astype(jnp.bfloat16)
            )

    def step(j, carry):
        whole = (j * block_k >= last_ref[index]) & ((j + 1) * block_k - 1 <= query_first)

        @pl.when(whole)
        def _():
            visit(j, False)

        @pl.when(jnp.logical_not(whole))
        def _():
            visit(j, True)

        return carry

    lax.fori_loop(low, high, step, 0)
    for head in range(heads_in):
        rows = slice(head * HEAD, (head + 1) * HEAD)
        weight = total[head : head + 1, :]
        tall_ref[rows, :] = summed[rows, :] / weight
        log_ref[0, head : head + 1, :] = best[head : head + 1, :] + jnp.log(weight)
    if heads_in * HEAD < LANES:
        tall_ref[heads_in * HEAD :, :] = jnp.zeros_like(tall_ref[heads_in * HEAD :, :])
    log_ref[0, heads_in:, :] = jnp.zeros_like(log_ref[0, heads_in:, :])
    out_ref[...] = tall_ref[...].T.astype(jnp.bfloat16)


def attend(pair, packed, slots, first, last, starts, heads_in, block_q, block_k, held):
    count, width = packed.shape
    pairs = width // 3 // LANES
    whole = pl.BlockSpec(memory_space=pl.ANY)
    return pl.pallas_call(
        partial(attend_kernel, block_q, block_k, heads_in),
        out_shape=(
            jax.ShapeDtypeStruct((count, pairs * LANES), jnp.bfloat16),
            jax.ShapeDtypeStruct((pairs * LANES, count), jnp.float32),
            jax.ShapeDtypeStruct((pairs, 8, count), jnp.float32),
        ),
        grid_spec=pltpu.PrefetchScalarGridSpec(
            num_scalar_prefetch=3,
            grid=(count // block_q,),
            in_specs=[
                pl.BlockSpec((1, block_q), lambda i, slots_ref, *_: (0, slots_ref[i])),
                pl.BlockSpec((block_q, LANES), lambda i, slots_ref, *_: (slots_ref[i], 3 * pair)),
                pl.BlockSpec((count, LANES), lambda i, *_: (0, 3 * pair + 1)),
                pl.BlockSpec((count, LANES), lambda i, *_: (0, 3 * pair + 2)),
            ]
            + [whole] * len(held),
            out_specs=(
                pl.BlockSpec((block_q, LANES), lambda i, slots_ref, *_: (slots_ref[i], pair)),
                pl.BlockSpec((LANES, block_q), lambda i, slots_ref, *_: (pair, slots_ref[i])),
                pl.BlockSpec((1, 8, block_q), lambda i, slots_ref, *_: (pair, 0, slots_ref[i])),
            ),
            scratch_shapes=[
                pltpu.VMEM((LANES, count), jnp.bfloat16),
                pltpu.VMEM((8, block_q), jnp.float32),
                pltpu.VMEM((8, block_q), jnp.float32),
                pltpu.VMEM((LANES, block_q), jnp.float32),
            ],
        ),
        input_output_aliases={7 + k: k for k in range(len(held))},
        cost_estimate=pl.CostEstimate(
            flops=2 * 2 * count * count * LANES,
            bytes_accessed=12 * count * LANES,
            transcendentals=2 * count * count,
        ),
        name="attend",
    )(slots, first, last, starts.reshape(1, count), packed, packed, packed, *held)


def attend_back_kernel(
    block_q,
    block_k,
    heads_in,
    slots_ref,
    last_ref,
    end_ref,
    start_ref,
    cos_ref,
    sin_ref,
    query_ref,
    key_ref,
    value_ref,
    tall_ref,
    log_ref,
    grad_ref,
    *refs,
):
    out_ref, turned, masked_q, masked_g, delta, tall_q, key_sum, value_sum = refs[-8:]
    index = pl.program_id(0)
    count = query_ref.shape[0]

    def turn_back(field, rows):
        return field * cos_ref[rows, :] - partner(field) * sin_ref[rows, :]

    @pl.when(index == 0)
    def _():
        def prepare(j, carry):
            rows = pl.ds(pl.multiple_of(j * block_k, block_k), block_k)
            turned[:, rows] = key_ref[rows, :].astype(jnp.float32).T.astype(jnp.bfloat16)
            grads = grad_ref[rows, :]
            product = grads.astype(jnp.float32).T * tall_ref[:, rows]
            for head in range(heads_in):
                masked_q[head, rows, :] = head_lanes(query_ref[rows, :], head)
                masked_g[head, rows, :] = head_lanes(grads, head)
                delta[head : head + 1, rows] = jnp.sum(
                    product[head * HEAD : (head + 1) * HEAD, :], axis=0, keepdims=True
                )
            tall_q[:, rows] = jnp.zeros((LANES, block_k), jnp.float32)
            return carry

        lax.fori_loop(0, count // block_k, prepare, 0)

    key_first = index * block_k
    key_rows = pl.ds(pl.multiple_of(slots_ref[index] * block_k, block_k), block_k)
    keys = key_ref[key_rows, :]
    values = value_ref[key_rows, :]
    key_sum[...] = jnp.zeros_like(key_sum)
    value_sum[...] = jnp.zeros_like(value_sum)

    def visit(i, masked):
        query_first = i * block_q
        rows = pl.ds(pl.multiple_of(slots_ref[i] * block_q, block_q), block_q)
        if masked:
            allowed = pair_allowed(
                start_ref[0:1, rows], key_first, block_k, query_first, block_q
            )
        for head in range(heads_in):
            queries = masked_q[head, rows, :]
            grads = masked_g[head, rows, :]
            scores = dot_last(keys, queries)
            probs = jnp.exp(scores - log_ref[0, head : head + 1, rows])
            if masked:
                probs = jnp.where(allowed, probs, 0.0)
            value_sum[...] += dot_plain(probs.astype(jnp.bfloat16), grads)
            prob_grad = dot_last(values, grads)
            score_grad = (probs * (prob_grad - delta[head : head + 1, rows])).astype(jnp.bfloat16)
            key_sum[...] += dot_plain(score_grad, queries)
            lanes = slice(head * HEAD, (head + 1) * HEAD)
            tall_q[lanes, rows] += dot_plain(turned[lanes, key_rows], score_grad)

    def step(i, carry):
        whole = (key_first >= last_ref[i]) & (key_first + block_k - 1 <= i * block_q)

        @pl.when(whole)
        def _():
            visit(i, False)

        @pl.when(jnp.logical_not(whole))
        def _():
            visit(i, True)

        return carry

    lax.fori_loop(key_first // block_q, (end_ref[index] - 1) // block_q + 1, step, 0)
    out_ref[key_rows, LANES : 2 * LANES] = turn_back(key_sum[...], key_rows).astype(jnp.bfloat16)
    out_ref[key_rows, 2 * LANES :] = value_sum[...].astype(jnp.bfloat16)

    @pl.when(index == pl.num_programs(0) - 1)
    def _():
        def finish(j, carry):
            rows = pl.ds(pl.multiple_of(j * block_k, block_k), block_k)
            field = tall_q[:, rows].T * HEAD ** (-0.5)
            out_ref[rows, :LANES] = turn_back(field, rows).astype(jnp.bfloat16)
            return carry

        lax.fori_loop(0, count // block_k, finish, 0)


def attend_back(
    pair, packed, slots, last, end, starts, cosine, sine, tall, logs, grads,
    heads_in, block_q, block_k, held,
):
    count, width = packed.shape
    whole = pl.BlockSpec(memory_space=pl.ANY)
    return pl.pallas_call(
        partial(attend_back_kernel, block_q, block_k, heads_in),
        out_shape=jax.ShapeDtypeStruct((count, width), jnp.bfloat16),
        grid_spec=pltpu.PrefetchScalarGridSpec(
            num_scalar_prefetch=3,
            grid=(count // block_k,),
            in_specs=[
                pl.BlockSpec((1, count), lambda i, *_: (0, 0)),
                pl.BlockSpec((count, LANES), lambda i, *_: (0, 0)),
                pl.BlockSpec((count, LANES), lambda i, *_: (0, 0)),
                pl.BlockSpec((count, LANES), lambda i, *_: (0, 3 * pair)),
                pl.BlockSpec((count, LANES), lambda i, *_: (0, 3 * pair + 1)),
                pl.BlockSpec((count, LANES), lambda i, *_: (0, 3 * pair + 2)),
                pl.BlockSpec((LANES, count), lambda i, *_: (pair, 0)),
                pl.BlockSpec((1, 8, count), lambda i, *_: (pair, 0, 0)),
                pl.BlockSpec((count, LANES), lambda i, *_: (0, pair)),
            ]
            + [whole] * len(held),
            out_specs=pl.BlockSpec((count, 3 * LANES), lambda i, *_: (0, pair)),
            scratch_shapes=[
                pltpu.VMEM((LANES, count), jnp.bfloat16),
                pltpu.VMEM((heads_in, count, LANES), jnp.bfloat16),
                pltpu.VMEM((heads_in, count, LANES), jnp.bfloat16),
                pltpu.VMEM((8, count), jnp.float32),
                pltpu.VMEM((LANES, count), jnp.float32),
                pltpu.VMEM((block_k, LANES), jnp.float32),
                pltpu.VMEM((block_k, LANES), jnp.float32),
            ],
        ),
        input_output_aliases={12 + k: k for k in range(len(held))},
        compiler_params=pltpu.CompilerParams(vmem_limit_bytes=60 << 20),
        cost_estimate=pl.CostEstimate(
            flops=5 * 2 * count * count * LANES,
            bytes_accessed=20 * count * LANES,
            transcendentals=2 * count * count,
        ),
        name="attend_back",
    )(
        slots, last, end, starts.reshape(1, count), cosine, sine,
        packed, packed, packed, tall, logs, grads, *held,
    )


def finish_kernel(narrow_count, wide_count, own_units, per_shard, *refs):
    exchange = own_units > 0
    if exchange:
        (
            parts_ref, piece_ref, total_ref, block_ref, near, far, near_sum,
            send_near, recv_near, send_far, recv_far, send_piece, recv_piece,
        ) = refs
    else:
        (
            parts_ref, total_ref, near, far, near_sum, send_near, recv_near, send_far, recv_far,
        ) = refs
    narrow_me = lax.axis_index("narrow")
    wide_me = lax.axis_index("wide")

    def place(narrow_at, wide_at):
        return {"narrow": narrow_at, "wide": wide_at}

    mesh_ids = pl.DeviceIdType.MESH
    barrier = pltpu.get_barrier_semaphore()
    greeted = 0
    for ahead in range(narrow_count):
        for across in range(wide_count):
            if (ahead > 0) + (across > 0) == 0 or (not exchange and ahead > 0 and across > 0):
                continue
            greeted += 1
            pl.semaphore_signal(
                barrier,
                inc=1,
                device_id=place(
                    lax.rem(narrow_me + ahead, narrow_count), lax.rem(wide_me + across, wide_count)
                ),
                device_id_type=mesh_ids,
            )
    pl.semaphore_wait(barrier, greeted)
    near_copies = []
    for ahead in range(1, narrow_count):
        copy = pltpu.make_async_remote_copy(
            src_ref=parts_ref,
            dst_ref=near.at[narrow_me],
            send_sem=send_near.at[ahead - 1],
            recv_sem=recv_near.at[ahead - 1],
            device_id=place(lax.rem(narrow_me + ahead, narrow_count), wide_me),
            device_id_type=mesh_ids,
        )
        copy.start()
        near_copies.append(copy)
    near[narrow_me] = parts_ref[...]
    if exchange:
        rows = piece_ref.shape[0]
        halves = block_ref.shape[0] // rows
        half_me = lax.rem(wide_me, halves)
        narrow_to = lax.div(wide_me, halves)
        moves = []
        for unit in range(3 * own_units):
            whole_unit = (unit % 3) * (D // LANES) + narrow_me * own_units + unit // 3
            wide_to = lax.div(whole_unit, per_shard)
            column = lax.rem(whole_unit, per_shard)
            source = piece_ref.at[:, unit * LANES : (unit + 1) * LANES]
            target = block_ref.at[
                pl.ds(pl.multiple_of(half_me * rows, rows), rows),
                pl.ds(pl.multiple_of(column * LANES, LANES), LANES),
            ]
            arrived = recv_piece.at[half_me * per_shard + column]
            remote = pltpu.make_async_remote_copy(
                src_ref=source,
                dst_ref=target,
                send_sem=send_piece.at[unit],
                recv_sem=arrived,
                device_id=place(narrow_to, wide_to),
                device_id_type=mesh_ids,
            )
            here = pltpu.make_async_copy(source, target, arrived)
            mine = (narrow_to == narrow_me) & (wide_to == wide_me)
            pl.when(jnp.logical_not(mine))(remote.start)
            pl.when(mine)(here.start)
            moves.append((mine, remote))
    for copy in near_copies:
        copy.wait()
    value = near[0]
    for k in range(1, narrow_count):
        value = value + near[k]
    near_sum[...] = value
    far_copies = []
    for across in range(1, wide_count):
        copy = pltpu.make_async_remote_copy(
            src_ref=near_sum,
            dst_ref=far.at[wide_me],
            send_sem=send_far.at[across - 1],
            recv_sem=recv_far.at[across - 1],
            device_id=place(narrow_me, lax.rem(wide_me + across, wide_count)),
            device_id_type=mesh_ids,
        )
        copy.start()
        far_copies.append(copy)
    far[wide_me] = value
    for copy in far_copies:
        copy.wait()
    value = far[0]
    for k in range(1, wide_count):
        value = value + far[k]
    total_ref[...] = value
    if exchange:
        for mine, remote in moves:
            pl.when(jnp.logical_not(mine))(remote.wait_send)
        for half in range(halves):
            for column in range(per_shard):
                pltpu.make_async_copy(
                    piece_ref.at[:, 0:LANES],
                    block_ref.at[
                        half * rows : (half + 1) * rows, column * LANES : (column + 1) * LANES
                    ],
                    recv_piece.at[half * per_shard + column],
                ).wait()


def finish(parts, piece, narrow_count, wide_count, own_width, proj_cols):
    shape = parts.shape
    exchange = piece is not None
    own_units = own_width // LANES if exchange else 0
    per_shard = proj_cols // LANES
    vmem = pl.BlockSpec(memory_space=pltpu.VMEM)
    shapes = [jax.ShapeDtypeStruct(shape, jnp.float32)]
    scratch = [
        pltpu.VMEM((narrow_count,) + shape, jnp.float32),
        pltpu.VMEM((wide_count,) + shape, jnp.float32),
        pltpu.VMEM(shape, jnp.float32),
        pltpu.SemaphoreType.DMA((narrow_count - 1,)),
        pltpu.SemaphoreType.DMA((narrow_count - 1,)),
        pltpu.SemaphoreType.DMA((wide_count - 1,)),
        pltpu.SemaphoreType.DMA((wide_count - 1,)),
    ]
    if exchange:
        shapes.append(jax.ShapeDtypeStruct((D // narrow_count, proj_cols), jnp.bfloat16))
        scratch += [
            pltpu.SemaphoreType.DMA((3 * own_units,)),
            pltpu.SemaphoreType.DMA((3 * own_units,)),
        ]
    return pl.pallas_call(
        partial(finish_kernel, narrow_count, wide_count, own_units, per_shard),
        out_shape=tuple(shapes),
        in_specs=[vmem] * len(shapes),
        out_specs=(vmem,) * len(shapes),
        scratch_shapes=scratch,
        compiler_params=pltpu.CompilerParams(collective_id=0, has_side_effects=True),
        name="finish",
    )(*([parts, piece] if exchange else [parts]))


def adam_update(
    weight, first_moment, second_moment, grad_value, step_rate, decay_coef, first_fix, second_fix
):
    new_first = beta_first * first_moment + (1.0 - beta_first) * grad_value
    new_second = beta_second * second_moment + (1.0 - beta_second) * grad_value * grad_value
    step_ratio = new_first / first_fix / (jnp.sqrt(new_second / second_fix) + adam_eps)
    return (weight - step_rate * (step_ratio + decay_coef * weight), new_first, new_second)


def shards(
    tokens,
    cotangent,
    seq_lengths,
    step_count,
    norm_params,
    norm_first,
    norm_second,
    proj_weight,
    proj_first,
    proj_second,
    merge_weight,
    merge_first,
    merge_second,
    up_weight,
    up_first,
    up_second,
    down_weight,
    down_first,
    down_second,
):
    tok_rows = tokens.shape[0]
    narrow_count = lax.axis_size("narrow")
    wide_count = lax.axis_size("wide")
    span_index = lax.axis_index("narrow")
    group_rows = tok_rows * narrow_count
    own_width = HEADS // narrow_count * HEAD
    held_width = max(own_width, LANES)
    heads_in = min(own_width, LANES) // HEAD
    shard_rows = D // narrow_count
    proj_cols = proj_weight.shape[1]
    lengths = seq_lengths[0]
    onward = [(i, (i + 1) % narrow_count) for i in range(narrow_count)]
    slots = lax.rem(
        span_index + narrow_count - jnp.arange(narrow_count, dtype=jnp.int32), narrow_count
    )

    def pad_lanes(array, axis):
        extra = [(0, 0)] * array.ndim
        extra[axis] = (0, held_width - own_width)
        return jnp.pad(array, extra) if held_width > own_width else array

    def meet(*values):
        return lax.optimization_barrier(values)

    def send_on(array):
        return lax.ppermute(array, "narrow", onward)

    def rows_of(array, slot):
        return array[slot * tok_rows : (slot + 1) * tok_rows]

    direct = own_width % LANES == 0 and proj_cols % LANES == 0 and merge_weight.shape[1] == LANES
    weight_part = jnp.concatenate(
        [proj_weight.astype(jnp.bfloat16), merge_weight.astype(jnp.bfloat16)], axis=1
    )
    weight_all = lax.all_gather(weight_part, ("narrow", "wide"), axis=0).reshape(
        narrow_count, wide_count, shard_rows, -1
    )
    up_slice = up_weight.astype(jnp.bfloat16)
    down_slice = down_weight.astype(jnp.bfloat16)

    places = (
        slots[:, None] * tok_rows + jnp.arange(tok_rows, dtype=jnp.int32)[None, :]
    ).reshape(group_rows)
    seq_start, unused = locate(lengths, places)
    cosine, sine = rotary_tables(places - seq_start)
    block_first = jnp.arange(narrow_count, dtype=jnp.int32) * tok_rows
    first_start, unused = locate(lengths, block_first)
    last_start, last_end = locate(lengths, block_first + (tok_rows - 1))

    token_blocks = [tokens]
    held = ()
    for slot in range(narrow_count - 1):
        moving = send_on(token_blocks[slot])
        held = feed(slot, narrow_count, token_blocks[slot], norm_params, up_slice, held)
        moving, *held = meet(moving, *held)
        token_blocks.append(moving)
    grad_first, last_block = meet(cotangent, token_blocks[-1])
    token_blocks[-1] = last_block
    grad_blocks = [grad_first]

    moving = send_on(grad_first)
    gathered, activated, slope = feed(
        narrow_count - 1, narrow_count, last_block, norm_params, up_slice, held
    )
    if direct:
        proj_own = pick_proj(weight_all, span_index, own_width)
        merge_turn = pick_merge(weight_all, slots, own_width)
    else:
        turned_all = jnp.transpose(weight_all, (0, 2, 1, 3))
        proj_copy = turned_all[..., :proj_cols].reshape(D, 3, narrow_count, own_width)
        proj_own = pad_lanes(
            lax.dynamic_index_in_dim(proj_copy, span_index, axis=2, keepdims=False), 2
        ).reshape(D, 3 * held_width)
        merge_copy = turned_all[..., proj_cols:].reshape(narrow_count, own_width, D)
        merge_turn = jnp.take(merge_copy, slots, axis=0).reshape(D, D)
    packed = project(gathered, proj_own, cosine, sine)
    moving, packed = meet(moving, packed)
    grad_blocks.append(moving)

    pairs = held_width // LANES
    attended_held = ()
    for hop in range(2, max(narrow_count, pairs + 2)):
        if hop < narrow_count:
            moving = send_on(grad_blocks[-1])
        if hop - 2 < pairs:
            attended_held = attend(
                hop - 2, packed, slots, first_start, last_start, seq_start,
                heads_in, tok_rows, tok_rows, attended_held,
            )
        moving, *attended_held = meet(moving, *attended_held)
        if hop < narrow_count:
            grad_blocks.append(moving)
    attended, tall, logs = attended_held
    grads_all = jnp.concatenate(grad_blocks, axis=0)

    def down_term(slot):
        return dot_plain(rows_of(activated, slot), down_slice)

    def wide_sum(grad):
        return lax.psum_scatter(grad, "wide", scatter_dimension=0, tiled=True)

    pieces = []
    for ahead in range(narrow_count):
        piece = rows_of(attended, (narrow_count - ahead) % narrow_count)[:, :own_width]
        if ahead > 0:
            piece = lax.ppermute(
                piece,
                "narrow",
                [(i, (i + ahead) % narrow_count) for i in range(narrow_count)],
            )
        pieces.append(piece)

    first_term = down_term(1).astype(jnp.bfloat16)
    first_term, grads_all = meet(first_term, grads_all)
    moving = send_on(first_term)
    hidden_grad = (dot_last(grads_all, down_slice) * slope).astype(jnp.bfloat16)
    down_grad = dot_first(activated, grads_all).astype(jnp.bfloat16)
    up_grad = dot_first(gathered, hidden_grad).astype(jnp.bfloat16)
    attended_grad = pad_lanes(
        dot_last(grads_all, merge_turn[:own_width]).astype(jnp.bfloat16), 1
    )
    moving, hidden_grad, attended_grad = meet(moving, hidden_grad, attended_grad)
    mixed_held = ()
    for hop in range(2, max(narrow_count, pairs + 2)):
        if hop < narrow_count:
            moving = send_on((moving.astype(jnp.float32) + down_term(hop)).astype(jnp.bfloat16))
        if hop - 2 < pairs:
            mixed_held = (
                attend_back(
                    hop - 2, packed, slots, last_start, last_end, seq_start, cosine, sine,
                    tall, logs, attended_grad, heads_in, tok_rows, tok_rows, mixed_held,
                ),
            )
        moving, *mixed_held = meet(moving, *mixed_held)
    (mixed_grad,) = mixed_held
    branch = moving.astype(jnp.float32) + down_term(0)
    merged = dot_plain(jnp.concatenate(pieces, axis=1), merge_turn)
    unit_rows, inv_std = normalize(tokens)
    output_rows = tokens.astype(jnp.float32) + merged + branch
    layer_out = output_rows.astype(jnp.bfloat16)

    terms = [None] * narrow_count
    norm_part = None
    for slot in list(range(1, narrow_count)) + [0]:
        terms[slot], sums = pull(
            slot, mixed_grad, hidden_grad, proj_own, up_slice, token_blocks[slot]
        )
        norm_part = sums if norm_part is None else norm_part + sums
    moving = terms[1].astype(jnp.bfloat16)
    for slot in list(range(2, narrow_count)) + [0]:
        normed_grad = send_on(moving).astype(jnp.float32) + terms[slot]
        moving = normed_grad.astype(jnp.bfloat16)
    unit_grad = normed_grad * norm_params[0]
    input_grad = cotangent.astype(jnp.float32) + inv_std * (
        unit_grad
        - jnp.mean(unit_grad, axis=1, keepdims=True)
        - unit_rows * jnp.mean(unit_grad * unit_rows, axis=1, keepdims=True)
    )

    part_rows = D // wide_count
    feed_part = wide_sum(
        jnp.concatenate(
            [
                up_grad.reshape(wide_count, part_rows, -1),
                down_grad.reshape(wide_count, part_rows, -1),
            ],
            axis=1,
        ).reshape(2 * D, -1)
    )
    proj_grad = dot_first(gathered, mixed_grad).astype(jnp.bfloat16)
    merge_grad = dot_first(grads_all, attended).astype(jnp.bfloat16)
    if not direct:
        proj_grad = proj_grad.reshape(D, 3, held_width)[:, :, :own_width].reshape(D, -1)
        merge_grad = merge_grad[:, :own_width]
    heads_part = wide_sum(jnp.concatenate([proj_grad, merge_grad], axis=1))
    merge_block = heads_part[:, 3 * own_width :].T.astype(jnp.float32)

    def squares(array):
        value = array.astype(jnp.float32)
        return jnp.sum(value * value)

    scalars = jnp.stack(
        [
            squares(heads_part) + squares(feed_part),
            squares(output_rows),
            squares(merged),
            squares(branch),
        ]
    )
    parts = jnp.concatenate(
        [norm_part.reshape(2 * D // LANES, LANES), jnp.pad(scalars, (0, LANES - 4))[None, :]]
    )
    parts = jnp.pad(parts, ((0, 7), (0, 0)))
    if direct:
        summed, proj_block = finish(
            parts, heads_part, narrow_count, wide_count, own_width, proj_cols
        )
        proj_block = proj_block.astype(jnp.float32)
    else:
        (summed,) = finish(parts, None, narrow_count, wide_count, own_width, proj_cols)
        cross = lax.all_gather(heads_part[:, : 3 * own_width], "narrow", axis=0).reshape(
            narrow_count, part_rows, 3, own_width
        )
        cross = jnp.transpose(cross, (1, 2, 0, 3)).reshape(part_rows, wide_count, proj_cols)
        cross = lax.all_to_all(jnp.transpose(cross, (1, 0, 2)), "wide", 0, 0)
        proj_block = lax.dynamic_slice_in_dim(
            cross.reshape(D, proj_cols), span_index * shard_rows, shard_rows, axis=0
        ).astype(jnp.float32)
    norm_total = summed[: 2 * D // LANES].reshape(2, D)
    square_total = summed[2 * D // LANES, 0:1]
    output_squares = summed[2 * D // LANES, 1:2]
    branch_squares = summed[2 * D // LANES, 2:4]
    feed_all = lax.all_gather(feed_part, "wide", axis=0).reshape(
        wide_count, 2, part_rows, -1
    ).astype(jnp.float32)
    up_sum = feed_all[:, 0].reshape(up_weight.shape)
    down_sum = feed_all[:, 1].reshape(down_weight.shape)
    grad_norm = jnp.sqrt(square_total + jnp.sum(norm_total * norm_total))
    clip_factor = jnp.minimum(1.0, math.sqrt(NPARAMS) / grad_norm)
    entry_count = wide_count * group_rows * D
    residual_rms = jnp.sqrt(output_squares / entry_count)
    branch_norms = jnp.sqrt(branch_squares / entry_count)
    step_value = step_count[0].astype(jnp.float32)
    first_fix = 1.0 - jnp.power(beta_first, step_value)
    second_fix = 1.0 - jnp.power(beta_second, step_value)
    ramp = jnp.minimum(1.0, step_value / warmup_steps)
    norm_clipped = norm_total * clip_factor
    new_norm = adam_update(
        norm_params,
        norm_first,
        norm_second,
        norm_clipped,
        norm_rate * ramp,
        0.0,
        first_fix,
        second_fix,
    )
    new_proj = adam_update(
        proj_weight,
        proj_first,
        proj_second,
        proj_block * clip_factor,
        matrix_rate * ramp,
        decay_rate,
        first_fix,
        second_fix,
    )
    new_merge = adam_update(
        merge_weight,
        merge_first,
        merge_second,
        merge_block * clip_factor,
        matrix_rate * ramp,
        decay_rate,
        first_fix,
        second_fix,
    )
    new_up = adam_update(
        up_weight,
        up_first,
        up_second,
        up_sum * clip_factor,
        matrix_rate * ramp,
        decay_rate,
        first_fix,
        second_fix,
    )
    new_down = adam_update(
        down_weight,
        down_first,
        down_second,
        down_sum * clip_factor,
        matrix_rate * ramp,
        decay_rate,
        first_fix,
        second_fix,
    )
    return (
        layer_out,
        input_grad,
        grad_norm,
        residual_rms,
        norm_clipped,
        new_norm[0],
        new_norm[1],
        new_norm[2],
        new_proj[0],
        new_proj[1],
        new_proj[2],
        new_merge[0],
        new_merge[1],
        new_merge[2],
        new_up[0],
        new_up[1],
        new_up[2],
        new_down[0],
        new_down[1],
        new_down[2],
        branch_norms,
        new_proj[0].astype(jnp.bfloat16),
        new_merge[0].astype(jnp.bfloat16),
        new_up[0].astype(jnp.bfloat16),
        new_down[0].astype(jnp.bfloat16),
    )


def solution(mesh):
    placed = (
        P(("wide", "narrow"), None),
        P(("wide", "narrow"), None),
        P("wide", None),
        P(),
        P(),
        P(),
        P(),
        P("narrow", "wide"),
        P("narrow", "wide"),
        P("narrow", "wide"),
        P("narrow", "wide"),
        P("narrow", "wide"),
        P("narrow", "wide"),
        P(None, "narrow"),
        P(None, "narrow"),
        P(None, "narrow"),
        P("narrow", None),
        P("narrow", None),
        P("narrow", None),
    )
    return jax.shard_map(
        shards,
        mesh=mesh,
        in_specs=placed,
        out_specs=(
            P(("wide", "narrow"), None),
            P(("wide", "narrow"), None),
            P(),
            P(),
            P(),
            P(),
            P(),
            P(),
            P("narrow", "wide"),
            P("narrow", "wide"),
            P("narrow", "wide"),
            P("narrow", "wide"),
            P("narrow", "wide"),
            P("narrow", "wide"),
            P(None, "narrow"),
            P(None, "narrow"),
            P(None, "narrow"),
            P("narrow", None),
            P("narrow", None),
            P("narrow", None),
            P(),
            P("narrow", "wide"),
            P("narrow", "wide"),
            P(None, "narrow"),
            P("narrow", None),
        ),
        check_vma=False,
    )
```

time: 1430 us -> 538 us (0.38)
  waiting for transfers between devices: 879 us -> 163 us
  matrix products: 299 us -> 59.1 us
  Pallas kernels: 0 us -> 176 us
  blocking collectives: 52.7 us -> 0 us
  local copies, waits for them, and re-layouts: 50 us -> 11.7 us
  other arithmetic: 108 us -> 93.1 us
    reduce_scatter x4 -> x2, waiting for transfers between devices: 273 us -> 0.02 us  [wide_sum(): return lax.psum_scatter(grad, 'wide', scatter_dimension=0, tiled=True)]
    dot_general x36 -> x11, matrix products: 299 us -> 59.1 us  [the longest x4 23.9 us: dot_first(): lax.dot_general(left_side, right_side, (((0,), (0,)), ((), ())), preferre...]
    ppermute x6 -> x15, waiting for transfers between devices: 370 us -> 162 us  [the longest x12 140 us: send_on(): return lax.ppermute(array, 'narrow', onward)]
    pallas_call x0 -> x16, Pallas kernels: none -> 176 us  [the longest x1 42.6 us: finish(): pl.pallas_call(partial(finish_kernel, narrow_count, wide_count, own_units...]
    all_gather x5 -> x2, waiting for transfers between devices: 169 us -> 0.01 us  [the longest x1 0.01 us: shards(): lax.all_gather(weight_part, ('narrow', 'wide'), axis=0)]
    unnamed x14 -> x4, waiting for transfers between devices: 67.3 us -> 0.55 us
    psum x1 -> x0, blocking collectives: 40.2 us -> none  [shards(): lax.psum((local_squares.reshape(1), norm_part, jnp.sum(output_rows * outp...]
    reduce_sum x9 -> x5, other arithmetic: 39.7 us -> 3.92 us  [the longest x2 2.56 us: squares(): return jnp.sum(value * value)]
  transfers between devices with their start and end apart: 18 -> 19, of which waited for: 13 -> 13; matrix products, arithmetic and copies ran while one was open for 30% -> 17% of each run, Pallas kernels for 0% -> 33%
where the time goes in v1:
time: 538 us; the launch traced here: 532 us
  Pallas kernels  176 us (33%)
  waiting for transfers between devices  163 us (30%)
  other arithmetic  93.1 us (17%)
  matrix products  59.1 us (11%)
  between operations  20.9 us (4%)
  local copies, waits for them, and re-layouts  11.7 us (2%)
  starting transfers between devices  8.22 us (2%)
    ppermute x12, waiting for transfers between devices, send_on(): return lax.ppermute(array, 'narrow', onward)  140 us
    pallas_call x1, Pallas kernels, finish(): pl.pallas_call(partial(finish_kernel, narrow_count, wide_count, own_units...  42.6 us
    pallas_call x2, Pallas kernels, attend_back(): pl.pallas_call(partial(attend_back_kernel, block_q, block_k, heads_in), o...  37.8 us
    pallas_call x2, Pallas kernels, attend(): pl.pallas_call(partial(attend_kernel, block_q, block_k, heads_in), out_sh...  28.4 us
    pallas_call x4, Pallas kernels, pull(): pl.pallas_call(pull_kernel, out_shape=(jax.ShapeDtypeStruct((rows, depth)...  24.8 us
    convert_element_type x1, other arithmetic, shards(): new_down[0].astype(jnp.bfloat16)  24 us
    dot_general x4, matrix products, dot_first(): lax.dot_general(left_side, right_side, (((0,), (0,)), ((), ())), preferre...  23.9 us
    dot_general x5, matrix products, dot_plain(): lax.dot_general(left_side, right_side, (((1,), (0,)), ((), ())), preferre...  23.1 us
  transfers between devices with their start and end apart: 19, of which 13 were waited for; matrix products, arithmetic and copies ran while one was open for 17% of the time, Pallas kernels for 33%

profile of v1, /device:TPU:0, one launch (start us, length us, event | category | flops | bytes accessed | tf_op | source)
XLA Modules:
  0.0 531.7 jit_solution(531012013484156924)
XLA Ops:
  22.5 21.6 %collective-permute-done.tokens_ref = bf16[512,1024]{1,0:T(8,128)(2,1)S(1)} collective-permute-done((bf16[512,1024]{1,0:T(8,128)(2,1)}, bf16[512,1024]{1,0:T(8,128)(2,1)S(1)}, u32[]{:S(2)}, u32[]{:S(2)}) %collective-permute-start) | collective-permute-done | bytes 1048608 | tf_op jit(solution)/shard_map/ppermute | solution.py:763
  50.7 30.8 %collective-permute-done.1.tokens_ref = bf16[512,1024]{1,0:T(8,128)(2,1)S(1)} collective-permute-done((bf16[512,1024]{1,0:T(8,128)(2,1)S(1)}, bf16[512,1024]{1,0:T(8,128)(2,1)S(1)}, u32[]{:S(2)}, u32[]{:S(2)}) %collective-permute-start.1) | collective-permute-done | bytes 1048608 | tf_op jit(solution)/shard_map/ppermute | solution.py:763
  88.1 39.7 %collective-permute-done.2.tokens_ref = bf16[512,1024]{1,0:T(8,128)(2,1)S(1)} collective-permute-done((bf16[512,1024]{1,0:T(8,128)(2,1)S(1)}, bf16[512,1024]{1,0:T(8,128)(2,1)S(1)}, u32[]{:S(2)}, u32[]{:S(2)}) %collective-permute-start.2) | collective-permute-done | bytes 1048608 | tf_op jit(solution)/shard_map/ppermute | solution.py:763
  143.9 8.2 %project.1.query_ref.key_ref.value_ref = bf16[2048,768]{1,0:T(8,128)(2,1)} custom-call(bf16[2048,1024]{1,0:T(8,128)(2,1)} %get-tuple-element.109.rows_ref, bf16[1024,768]{1,0:T(8,128)(2,1)} %pick_proj.1.weight_ref.proj_ref, f32[2048,128]{1,0:T(8,128)} %get-tuple-element.262.cos_ref, f32[2048,128]{1,0:T(8,128)} %get-tuple-element.261.sin_ref), custom_call_target="tpu_custom_call" | custom-call | flops 3221225472 | bytes 8912896 | tf_op jit(solution)/shard_map/project/pallas_call | solution.py:98
  156.1 14.1 %attend.2 = (bf16[2048,256]{1,0:T(8,128)(2,1)}, f32[256,2048]{1,0:T(8,128)}, f32[2,8,2048]{2,1,0:T(8,128)}) custom-call(s32[4]{0:T(128)} %compare_select_fusion.slots_ref, s32[4]{0:T(128)} %select_reduce_fusion.3.first_ref, s32[4]{0:T(128)} %get-tuple-element.232.last_ref, s32[1,2048]{1,0:T(1,128)} %bitcast.71, ...), custom_call_target="tpu_custom_call" | custom-call | flops 2147483648 | bytes 3145728 | tf_op jit(solution)/shard_map/attend/pallas_call | solution.py:373
  170.2 9.1 %collective-permute-done.4 = bf16[512,1024]{1,0:T(8,128)(2,1)} collective-permute-done((bf16[512,1024]{1,0:T(8,128)(2,1)S(1)}, bf16[512,1024]{1,0:T(8,128)(2,1)}, u32[]{:S(2)}, u32[]{:S(2)}) %collective-permute-start.4) | collective-permute-done | bytes 1048608 | tf_op jit(solution)/shard_map/ppermute | solution.py:763
  186.1 14.3 %attend.3 = (bf16[2048,256]{1,0:T(8,128)(2,1)}, f32[256,2048]{1,0:T(8,128)}, f32[2,8,2048]{2,1,0:T(8,128)}) custom-call(s32[4]{0:T(128)} %compare_select_fusion.slots_ref, s32[4]{0:T(128)} %select_reduce_fusion.3.first_ref, s32[4]{0:T(128)} %get-tuple-element.232.last_ref, ...), custom_call_target="tpu_custom_call", output_to_operand_aliasing={{0}: (7, {}), {1}: (8, {}), {2}: (9, {})} | custom-call | flops 2147483648 | bytes 3145728 | tf_op jit(solution)/shard_map/attend/pallas_call | solution.py:373
  213.0 6.8 %fusion.49 = f32[2048,1024]{1,0:T(8,128)} fusion(bf16[2048,1024]{1,0:T(8,128)(2,1)S(1)} %pad_maximum_fusion, bf16[1024,1024]{1,0:T(8,128)(2,1)S(1)} %convert_element_type.139), kind=kOutput, calls=%fused_computation.126 | convolution fusion | flops 4294967296 | bytes 14680064 | tf_op jit(solution)/shard_map/dot_general | solution.py:32
  219.8 7.3 %multiply_convert_fusion.hidden_ref = bf16[2048,1024]{1,0:T(8,128)(2,1)S(1)} fusion(f32[2048,1024]{1,0:T(8,128)} %fusion.49, f32[2048,1024]{1,0:T(8,128)} %get-tuple-element.127), kind=kLoop, calls=%fused_computation | loop fusion | flops 4194304 | bytes 20971520 | tf_op jit(solution)/shard_map/convert_element_type | solution.py:853
  227.1 8.5 %convolution_convert_fusion.2 = bf16[1024,1024]{1,0:T(8,128)(2,1)S(1)} fusion(bf16[2048,1024]{1,0:T(8,128)(2,1)} %get-tuple-element.109.rows_ref, bf16[2048,1024]{1,0:T(8,128)(2,1)S(1)} %multiply_convert_fusion.hidden_ref), kind=kOutput, calls=%fused_computation.38 | convolution fusion | flops 4296015872 | bytes 10485760 | tf_op jit(solution)/shard_map/dot_general | solution.py:44
  243.6 6.9 %pick_merge.1 = bf16[1024,1024]{1,0:T(8,128)(2,1)} custom-call(s32[4]{0:T(128)} %compare_select_fusion.slots_ref, bf16[4,8,256,512]{3,2,1,0:T(8,128)(2,1)} %bitcast.66), custom_call_target="tpu_custom_call" | custom-call | bytes 4194304 | tf_op jit(solution)/shard_map/pick_merge/pallas_call | solution.py:257
  255.8 6.4 %collective-permute-done.9 = bf16[512,1024]{1,0:T(8,128)(2,1)} collective-permute-done((bf16[512,1024]{1,0:T(8,128)(2,1)}, bf16[512,1024]{1,0:T(8,128)(2,1)}, u32[]{:S(2)}, u32[]{:S(2)}) %collective-permute-start.9) | collective-permute-done | bytes 1048608 | tf_op jit(solution)/shard_map/ppermute | solution.py:763
  268.7 18.9 %attend_back.2.refs_0_ = bf16[2048,768]{1,0:T(8,128)(2,1)} custom-call(s32[4]{0:T(128)} %compare_select_fusion.slots_ref, s32[4]{0:T(128)} %get-tuple-element.232.last_ref, s32[4]{0:T(128)} %get-tuple-element.230.end_ref, s32[1,2048]{1,0:T(1,128)} %bitcast.73, f32[2048,128]{1,0:T(8,128)} %get-tuple-element.262.cos_ref, ...), custom_call_target="tpu_custom_call" | custom-call | flops 5368709120 | bytes 5242880 | tf_op jit(solution)/shard_map/attend_back/pallas_call | solution.py:517
  293.1 18.9 %attend_back.3.mixed_ref = bf16[2048,768]{1,0:T(8,128)(2,1)} custom-call(s32[4]{0:T(128)} %compare_select_fusion.slots_ref, s32[4]{0:T(128)} %get-tuple-element.232.last_ref, s32[4]{0:T(128)} %get-tuple-element.230.end_ref, s32[1,2048]{1,0:T(1,128)} %bitcast.74, f32[2048,128]{1,0:T(8,128)} %get-tuple-element.262.cos_ref, ...), custom_call_target="tpu_custom_call", output_to_operand_aliasing={{}: (12, {})} | custom-call | flops 5368709120 | bytes 5242880 | tf_op jit(solution)/shard_map/attend_back/pallas_call | solution.py:517
  313.1 7.0 %convolution_convert_fusion.3 = bf16[1024,768]{1,0:T(8,128)(2,1)S(1)} fusion(bf16[2048,1024]{1,0:T(8,128)(2,1)} %get-tuple-element.109.rows_ref, bf16[2048,768]{1,0:T(8,128)(2,1)} %attend_back.3.mixed_ref), kind=kOutput, calls=%fused_computation.39 | convolution fusion | flops 3222011904 | bytes 8912896 | tf_op jit(solution)/shard_map/dot_general | solution.py:44
  336.4 15.5 %collective-permute-done.12 = bf16[512,1024]{1,0:T(8,128)(2,1)} collective-permute-done((bf16[512,1024]{1,0:T(8,128)(2,1)S(1)}, bf16[512,1024]{1,0:T(8,128)(2,1)}, u32[]{:S(2)}, u32[]{:S(2)}) %collective-permute-start.12) | collective-permute-done | bytes 1048608 | tf_op jit(solution)/shard_map/ppermute | solution.py:763
  358.6 6.4 %pull.6 = (f32[512,1024]{1,0:T(8,128)}, f32[2,1024]{1,0:T(2,128)}) custom-call(bf16[2048,768]{1,0:T(8,128)(2,1)} %attend_back.3.mixed_ref, bf16[2048,1024]{1,0:T(8,128)(2,1)} %copy-done, bf16[1024,768]{1,0:T(8,128)(2,1)} %pick_proj.1.weight_ref.proj_ref, bf16[1024,1024]{1,0:T(8,128)(2,1)} %convert_element_type.132.weight_ref.up_ref, bf16[512,1024]{1,0:T(8,128)(2,1)} %copy-done.4), custom_call_target="tpu_custom_call" | custom-call | flops 1879048192 | bytes 7864320 | tf_op jit(solution)/shard_map/pull/pallas_call | solution.py:192
  365.0 10.1 %collective-permute-done.13 = bf16[512,1024]{1,0:T(8,128)(2,1)} collective-permute-done((bf16[512,1024]{1,0:T(8,128)(2,1)S(1)}, bf16[512,1024]{1,0:T(8,128)(2,1)}, u32[]{:S(2)}, u32[]{:S(2)}) %collective-permute-start.13) | collective-permute-done | bytes 1048608 | tf_op jit(solution)/shard_map/ppermute | solution.py:763
  387.3 6.1 %pull.7 = (f32[512,1024]{1,0:T(8,128)}, f32[2,1024]{1,0:T(2,128)}) custom-call(bf16[2048,768]{1,0:T(8,128)(2,1)} %attend_back.3.mixed_ref, bf16[2048,1024]{1,0:T(8,128)(2,1)} %copy-done, bf16[1024,768]{1,0:T(8,128)(2,1)} %pick_proj.1.weight_ref.proj_ref, bf16[1024,1024]{1,0:T(8,128)(2,1)} %convert_element_type.132.weight_ref.up_ref, bf16[512,1024]{1,0:T(8,128)(2,1)} %tokens_ref.3), custom_call_target="tpu_custom_call" | custom-call | flops 1879048192 | bytes 7864320 | tf_op jit(solution)/shard_map/pull/pallas_call | solution.py:192
  398.6 7.1 %collective-permute-done.8 = bf16[512,256]{1,0:T(8,128)(2,1)} collective-permute-done((bf16[512,256]{1,0:T(8,128)(2,1)}, bf16[512,256]{1,0:T(8,128)(2,1)}, u32[]{:S(2)}, u32[]{:S(2)}) %collective-permute-start.8) | collective-permute-done | bytes 262176 | tf_op jit(solution)/shard_map/ppermute | solution.py:843
  405.8 15.2 %collective-permute-done.7 = bf16[512,256]{1,0:T(8,128)(2,1)} collective-permute-done((bf16[512,256]{1,0:T(8,128)(2,1)}, bf16[512,256]{1,0:T(8,128)(2,1)}, u32[]{:S(2)}, u32[]{:S(2)}) %collective-permute-start.7) | collective-permute-done | bytes 262176 | tf_op jit(solution)/shard_map/ppermute | solution.py:843
  421.0 7.3 %fusion.28 = (f32[512]{0:T(512)S(1)}, f32[512]{0:T(512)S(1)}, f32[]{:T(128)}, f32[]{:T(128)}, f32[]{:T(128)}, /*index=5*/bf16[512,1024]{1,0:T(8,128)(2,1)}) fusion(f32[1024]{0:T(1024)} %bitcast.77, f32[512,1024]{1,0:T(8,128)} %get-tuple-element.140, bf16[512,1024]{1,0:T(8,128)(2,1)} %collective-permute-done.14, f32[512]{0:T(512)} %add_rsqrt_fusion, ...), kind=kOutput, calls=%fused_computation.63 | convolution fusion | flops 1088420864 | bytes 11546636 | tf_op jit(solution)/shard_map/dot_general | solution.py:38
  431.0 42.6 %finish.1 = (f32[24,128]{1,0:T(8,128)}, bf16[256,384]{1,0:T(8,128)(2,1)}) custom-call(f32[24,128]{1,0:T(8,128)} %select_maximum_fusion.refs_0_, bf16[128,1024]{1,0:T(8,128)(2,1)} %reduce-scatter.3.cloned.1.call-done.refs_1_), custom_call_target="tpu_custom_call" | custom-call | tf_op jit(solution)/shard_map/finish/pallas_call | solution.py:697
  498.6 24.0 %fusion.38 = (bf16[1024,1024]{1,0:T(8,128)(2,1)}, f32[1024,1024]{1,0:T(8,128)}, f32[1024,1024]{1,0:T(8,128)}, f32[1024,1024]{1,0:T(8,128)}, bf16[1024,1024]{1,0:...) fusion(f32[1024,1024]{1,0:T(8,128)} %param.35, f32[]{:T(128)} %bitcast.21, ...), kind=kLoop, calls=%fused_computation.120 | loop fusion | flops 31457280 | bytes 62914568 | tf_op jit(solution)/shard_map/convert_element_type | solution.py:1040
  (182 shorter events, 158.1 us)
Async XLA Ops:
  7.2 132.0 %all-gather.5.cloned.1.call-start = ((), (), s32[]{:S(2)}) async-start(), calls=%async_computation.4 | async-start | bytes 8650752 | tf_op jit(solution)/shard_map/all_gather | solution.py:772
  9.9 311.9 %reduce-scatter.5.cloned.1.call-start = ((), (), s32[]{:S(2)}) async-start(), calls=%async_computation.3 | async-start | bytes 4718592 | tf_op jit(solution)/shard_map/reduce_scatter | solution.py:837
  10.0 34.1 %collective-permute-start = (bf16[512,1024]{1,0:T(8,128)(2,1)}, bf16[512,1024]{1,0:T(8,128)(2,1)S(1)}, u32[]{:S(2)}, u32[]{:S(2)}) collective-permute-start(bf16[512,1024]{1,0:T(8,128)(2,1)} %tokens_ref.3), channel_id=1, source_target_pairs={{0,1},{1,2},{2,3},{3,0},{4,5},{5,6},{6,7},{7,4},{8,9},{9,10},{10,1... | collective-permute-start | bytes 3145736 | tf_op jit(solution)/shard_map/ppermute | solution.py:763
  44.1 37.4 %collective-permute-start.1 = (bf16[512,1024]{1,0:T(8,128)(2,1)S(1)}, bf16[512,1024]{1,0:T(8,128)(2,1)S(1)}, u32[]{:S(2)}, u32[]{:S(2)}) collective-permute-start(bf16[512,1024]{1,0:T(8,128)(2,1)S(1)} %collective-permute-done.tokens_ref), channel_id=1, source_target_pairs={{0,1},{1,2},{2,3},{3,0},{4,5},{5,6},{6,7},{7,4},{8,9},{9,10},{10,1... | collective-permute-start | bytes 3145736 | tf_op jit(solution)/shard_map/ppermute | solution.py:763
  81.5 46.4 %collective-permute-start.2 = (bf16[512,1024]{1,0:T(8,128)(2,1)S(1)}, bf16[512,1024]{1,0:T(8,128)(2,1)S(1)}, u32[]{:S(2)}, u32[]{:S(2)}) collective-permute-start(bf16[512,1024]{1,0:T(8,128)(2,1)S(1)} %collective-permute-done.1.tokens_ref), channel_id=1, source_target_pairs={{0,1},{1,2},{2,3},{3,0},{4,5},{5,6},{6,7},{7,4},{8,9},{9,10},{10,1... | collective-permute-start | bytes 3145736 | tf_op jit(solution)/shard_map/ppermute | solution.py:763
  127.8 26.1 %collective-permute-start.3 = (bf16[512,1024]{1,0:T(8,128)(2,1)S(1)}, bf16[512,1024]{1,0:T(8,128)(2,1)S(1)}, u32[]{:S(2)}, u32[]{:S(2)}) collective-permute-start(bf16[512,1024]{1,0:T(8,128)(2,1)S(1)} %copy-done.9), channel_id=1, source_target_pairs={{0,1},{1,2},{2,3},{3,0},{4,5},{5,6},{6,7},{7,4},{8,9},{9,10},{10,1... | collective-permute-start | bytes 3145736 | tf_op jit(solution)/shard_map/ppermute | solution.py:763
  154.0 25.4 %collective-permute-start.4 = (bf16[512,1024]{1,0:T(8,128)(2,1)S(1)}, bf16[512,1024]{1,0:T(8,128)(2,1)}, u32[]{:S(2)}, u32[]{:S(2)}) collective-permute-start(bf16[512,1024]{1,0:T(8,128)(2,1)S(1)} %collective-permute-done.3), channel_id=1, source_target_pairs={{0,1},{1,2},{2,3},{3,0},{4,5},{5,6},{6,7},{7,4},{8,9},{9,10},{10,1... | collective-permute-start | bytes 3145736 | tf_op jit(solution)/shard_map/ppermute | solution.py:763
  179.3 24.7 %collective-permute-start.5 = (bf16[512,1024]{1,0:T(8,128)(2,1)}, bf16[512,1024]{1,0:T(8,128)(2,1)}, u32[]{:S(2)}, u32[]{:S(2)}) collective-permute-start(bf16[512,1024]{1,0:T(8,128)(2,1)} %collective-permute-done.4), channel_id=1, source_target_pairs={{0,1},{1,2},{2,3},{3,0},{4,5},{5,6},{6,7},{7,4},{8,9},{9,10},{10,1... | collective-permute-start | bytes 3145736 | tf_op jit(solution)/shard_map/ppermute | solution.py:763
  238.1 157.5 %reduce-scatter.3.cloned.1.call-start = ((), (), s32[]{:S(2)}) async-start(), calls=%async_computation.2 | async-start | bytes 2359296 | tf_op jit(solution)/shard_map/reduce_scatter | solution.py:837
  238.2 23.9 %collective-permute-start.9 = (bf16[512,1024]{1,0:T(8,128)(2,1)}, bf16[512,1024]{1,0:T(8,128)(2,1)}, u32[]{:S(2)}, u32[]{:S(2)}) collective-permute-start(bf16[512,1024]{1,0:T(8,128)(2,1)} %convolution_convert_fusion.4), channel_id=1, source_target_pairs={{0,1},{1,2},{2,3},{3,0},{4,5},{5,6},{6,7},{7,4},{8,9},{9,10},{10,1... | collective-permute-start | bytes 3145736 | tf_op jit(solution)/shard_map/ppermute | solution.py:763
  264.9 22.8 %collective-permute-start.10 = (bf16[512,1024]{1,0:T(8,128)(2,1)}, bf16[512,1024]{1,0:T(8,128)(2,1)}, u32[]{:S(2)}, u32[]{:S(2)}) collective-permute-start(bf16[512,1024]{1,0:T(8,128)(2,1)} %add_convert_fusion.3), channel_id=1, source_target_pairs={{0,1},{1,2},{2,3},{3,0},{4,5},{5,6},{6,7},{7,4},{8,9},{9,10},{10,1... | collective-permute-start | bytes 3145736 | tf_op jit(solution)/shard_map/ppermute | solution.py:763
  290.5 22.6 %collective-permute-start.11 = (bf16[512,1024]{1,0:T(8,128)(2,1)}, bf16[512,1024]{1,0:T(8,128)(2,1)S(1)}, u32[]{:S(2)}, u32[]{:S(2)}) collective-permute-start(bf16[512,1024]{1,0:T(8,128)(2,1)} %add_convert_fusion.2), channel_id=1, source_target_pairs={{0,1},{1,2},{2,3},{3,0},{4,5},{5,6},{6,7},{7,4},{8,9},{9,10},{10,1... | collective-permute-start | bytes 3145736 | tf_op jit(solution)/shard_map/ppermute | solution.py:763
  321.8 169.4 %all-gather.7.cloned.1.call-start = ((), (), s32[]{:S(2)}) async-start(), calls=%async_computation.5 | async-start | bytes 4718592 | tf_op jit(solution)/shard_map/all_gather | solution.py:950
  330.2 21.7 %collective-permute-start.12 = (bf16[512,1024]{1,0:T(8,128)(2,1)S(1)}, bf16[512,1024]{1,0:T(8,128)(2,1)}, u32[]{:S(2)}, u32[]{:S(2)}) collective-permute-start(bf16[512,1024]{1,0:T(8,128)(2,1)S(1)} %convert_element_type.150), channel_id=1, source_target_pairs={{0,1},{1,2},{2,3},{3,0},{4,5},{5,6},{6,7},{7,4},{8,9},{9,10},{10,1... | collective-permute-start | bytes 3145736 | tf_op jit(solution)/shard_map/ppermute | solution.py:763
  354.1 20.9 %collective-permute-start.13 = (bf16[512,1024]{1,0:T(8,128)(2,1)S(1)}, bf16[512,1024]{1,0:T(8,128)(2,1)}, u32[]{:S(2)}, u32[]{:S(2)}) collective-permute-start(bf16[512,1024]{1,0:T(8,128)(2,1)S(1)} %add_convert_fusion.1), channel_id=1, source_target_pairs={{0,1},{1,2},{2,3},{3,0},{4,5},{5,6},{6,7},{7,4},{8,9},{9,10},{10,1... | collective-permute-start | bytes 3145736 | tf_op jit(solution)/shard_map/ppermute | solution.py:763
  378.2 42.8 %collective-permute-start.14 = (bf16[512,1024]{1,0:T(8,128)(2,1)}, bf16[512,1024]{1,0:T(8,128)(2,1)}, u32[]{:S(2)}, u32[]{:S(2)}) collective-permute-start(bf16[512,1024]{1,0:T(8,128)(2,1)} %add_convert_fusion), channel_id=1, source_target_pairs={{0,1},{1,2},{2,3},{3,0},{4,5},{5,6},{6,7},{7,4},{8,9},{9,10},{10,1... | collective-permute-start | bytes 3145736 | tf_op jit(solution)/shard_map/ppermute | solution.py:763
  383.0 22.8 %collective-permute-start.8 = (bf16[512,256]{1,0:T(8,128)(2,1)}, bf16[512,256]{1,0:T(8,128)(2,1)}, u32[]{:S(2)}, u32[]{:S(2)}) collective-permute-start(bf16[512,256]{1,0:T(8,128)(2,1)} %get-tuple-element.256), channel_id=1, source_target_pairs={{0,3},{1,0},{2,1},{3,2},{4,7},{5,4},{6,5},{7,6},{8,11},{9,8},{10,9... | collective-permute-start | bytes 786440 | tf_op jit(solution)/shard_map/ppermute | solution.py:843
  386.7 34.3 %collective-permute-start.7 = (bf16[512,256]{1,0:T(8,128)(2,1)}, bf16[512,256]{1,0:T(8,128)(2,1)}, u32[]{:S(2)}, u32[]{:S(2)}) collective-permute-start(bf16[512,256]{1,0:T(8,128)(2,1)} %get-tuple-element.257), channel_id=1, source_target_pairs={{0,2},{1,3},{2,0},{3,1},{4,6},{5,7},{6,4},{7,5},{8,10},{9,11},{10,... | collective-permute-start | bytes 786440 | tf_op jit(solution)/shard_map/ppermute | solution.py:843
  386.7 34.3 %collective-permute-start.6 = (bf16[512,256]{1,0:T(8,128)(2,1)S(1)}, bf16[512,256]{1,0:T(8,128)(2,1)}, u32[]{:S(2)}, u32[]{:S(2)}) collective-permute-start(bf16[512,256]{1,0:T(8,128)(2,1)S(1)} %get-tuple-element.258), channel_id=1, source_target_pairs={{0,1},{1,2},{2,3},{3,0},{4,5},{5,6},{6,7},{7,4},{8,9},{9,10},{10,1... | collective-permute-start | bytes 786440 | tf_op jit(solution)/shard_map/ppermute | solution.py:843
  421.0 63.5 %copy-start.30 = (f32[2,1024]{1,0:T(2,128)S(1)}, f32[2,1024]{1,0:T(2,128)}, u32[]{:S(2)}) copy-start(f32[2,1024]{1,0:T(2,128)} %param.25) | copy-start | bytes 24580
  421.0 63.4 %copy-start.31 = (f32[2,1024]{1,0:T(2,128)S(1)}, f32[2,1024]{1,0:T(2,128)}, u32[]{:S(2)}) copy-start(f32[2,1024]{1,0:T(2,128)} %param.24) | copy-start | bytes 24580
  421.0 64.1 %copy-start.18 = (f32[256,384]{1,0:T(8,128)S(1)}, f32[256,384]{1,0:T(8,128)}, u32[]{:S(2)}) copy-start(f32[256,384]{1,0:T(8,128)} %param.26) | copy-start | bytes 1179652
  428.3 59.3 %copy-start.29 = (f32[1,1024]{1,0:T(1,128)S(1)}, f32[1,1024]{1,0:T(1,128)}, u32[]{:S(2)}) copy-start(f32[1,1024]{1,0:T(1,128)} %slice.60) | copy-start | bytes 12292
  428.3 59.3 %copy-start.32 = (f32[512]{0:T(512)S(1)}, f32[512]{0:T(512)}, u32[]{:S(2)}) copy-start(f32[512]{0:T(512)} %add_rsqrt_fusion) | copy-start | bytes 6148
  (30 other events, 434.2 us)
Sparse Core Ops, SparseCore 0:
  11.4 113.6 all-gather.4
  238.2 53.8 reduce-scatter.4
  321.9 52.4 reduce-scatter.2
  376.1 36.5 all-gather.6

commit v2 on v1

--- a/solution.py
+++ b/solution.py
@@ -26,6 +26,7 @@
 norm_rate = 1.0
 warmup_steps = 20.0
 masked_score = -1e30
+short = pl.CostEstimate(flops=0, bytes_accessed=0, transcendentals=0)
 
 
 def dot_last(left_side, right_side):
@@ -106,11 +107,7 @@
             pl.BlockSpec((block, LANES), lambda i: (i, 0)),
         ],
         out_specs=pl.BlockSpec((block, width), lambda i: (i, 0)),
-        cost_estimate=pl.CostEstimate(
-            flops=2 * count * depth * width,
-            bytes_accessed=2 * (count * depth + depth * width + count * width),
-            transcendentals=0,
-        ),
+        cost_estimate=short,
         name="project",
     )(rows, weight, cosine, sine)
 
@@ -160,13 +157,49 @@
             pl.BlockSpec((rows // 2, width), lambda i: (2 * slot + i, 0)),
         ),
         input_output_aliases={3 + k: k for k in range(len(held))},
-        cost_estimate=pl.CostEstimate(
-            flops=2 * rows * depth * width,
-            bytes_accessed=4 * rows * depth + 2 * depth * width + 6 * rows * width,
-            transcendentals=2 * rows * width,
-        ),
+        cost_estimate=short,
         name="feed",
     )(tokens, params, weight, *held)
+
+
+def push_kernel(grad_ref, slope_ref, down_ref, merge_ref, *refs):
+    all_ref, hidden_ref, attended_ref = refs[-3:]
+    grads = grad_ref[...]
+    all_ref[...] = grads
+    hidden_ref[...] = (dot_last(grads, down_ref[...]) * slope_ref[...]).astype(jnp.bfloat16)
+    attended_ref[...] = dot_last(grads, merge_ref[...]).astype(jnp.bfloat16)
+
+
+def push(slot, slots, grads, slope, down, merge, held):
+    rows, depth = grads.shape
+    width = slope.shape[1]
+    own = merge.shape[0]
+    half = rows // 2
+    whole = pl.BlockSpec(memory_space=pl.ANY)
+    return pl.pallas_call(
+        push_kernel,
+        out_shape=(
+            jax.ShapeDtypeStruct((slots * rows, depth), jnp.bfloat16),
+            jax.ShapeDtypeStruct((slots * rows, width), jnp.bfloat16),
+            jax.ShapeDtypeStruct((slots * rows, own), jnp.bfloat16),
+        ),
+        grid=(2,),
+        in_specs=[
+            pl.BlockSpec((half, depth), lambda i: (i, 0)),
+            pl.BlockSpec((half, width), lambda i: (2 * slot + i, 0)),
+            pl.BlockSpec(down.shape, lambda i: (0, 0)),
+            pl.BlockSpec(merge.shape, lambda i: (0, 0)),
+        ]
+        + [whole] * len(held),
+        out_specs=(
+            pl.BlockSpec((half, depth), lambda i: (2 * slot + i, 0)),
+            pl.BlockSpec((half, width), lambda i: (2 * slot + i, 0)),
+            pl.BlockSpec((half, own), lambda i: (2 * slot + i, 0)),
+        ),
+        input_output_aliases={4 + k: k for k in range(len(held))},
+        cost_estimate=short,
+        name="push",
+    )(grads, slope, down, merge, *held)
 
 
 def pull_kernel(mixed_ref, hidden_ref, proj_ref, up_ref, tokens_ref, out_ref, sums_ref):
@@ -207,11 +240,7 @@
             pl.BlockSpec((half, depth), lambda i: (i, 0)),
             pl.BlockSpec((2, depth), lambda i: (0, 0)),
         ),
-        cost_estimate=pl.CostEstimate(
-            flops=2 * rows * depth * (mixed.shape[1] + hidden_grad.shape[1]),
-            bytes_accessed=8 * rows * depth + 2 * depth * (proj.shape[1] + up.shape[1]),
-            transcendentals=0,
-        ),
+        cost_estimate=short,
         name="pull",
     )(mixed, hidden_grad, proj, up, tokens)
 
@@ -221,14 +250,14 @@
 
 
 def pick_proj(weight_all, span_index, own_width):
-    narrow_count, shards, rows, cols = weight_all.shape
+    shards, narrow_count, rows, cols = weight_all.shape
     units = own_width // LANES
-    per_shard = cols // LANES - 1
+    per_shard = cols // LANES
     per_part = D // LANES
 
     def source(c, index_ref):
         unit = (c % 3) * per_part + index_ref[0] * units + c // 3
-        return (0, unit // per_shard, 0, unit % per_shard)
+        return (unit // per_shard, 0, 0, unit % per_shard)
 
     return pl.pallas_call(
         pick_kernel,
@@ -236,24 +265,22 @@
         grid_spec=pltpu.PrefetchScalarGridSpec(
             num_scalar_prefetch=1,
             grid=(3 * units,),
-            in_specs=[pl.BlockSpec((narrow_count, 1, rows, LANES), source)],
+            in_specs=[pl.BlockSpec((1, narrow_count, rows, LANES), source)],
             out_specs=pl.BlockSpec((D, LANES), lambda c, index_ref: (0, c)),
         ),
-        cost_estimate=pl.CostEstimate(
-            flops=0, bytes_accessed=12 * D * own_width, transcendentals=0
-        ),
+        cost_estimate=short,
         name="pick_proj",
     )(span_index.reshape(1), weight_all)
 
 
 def turn_kernel(slots_ref, all_ref, out_ref):
-    narrow_count, unused, rows, cols = all_ref.shape
+    unused, narrow_count, rows, cols = all_ref.shape
     for t in range(narrow_count):
-        out_ref[t * rows : (t + 1) * rows, :] = all_ref[slots_ref[t], 0]
+        out_ref[t * rows : (t + 1) * rows, :] = all_ref[0, slots_ref[t]]
 
 
 def pick_merge(weight_all, slots, own_width):
-    narrow_count, shards, rows, cols = weight_all.shape
+    shards, narrow_count, rows, cols = weight_all.shape
     return pl.pallas_call(
         turn_kernel,
         out_shape=jax.ShapeDtypeStruct((D, D), jnp.bfloat16),
@@ -262,13 +289,13 @@
             grid=(shards,),
             in_specs=[
                 pl.BlockSpec(
-                    (narrow_count, 1, rows, LANES),
-                    lambda j, slots_ref: (0, j, 0, cols // LANES - 1),
+                    (1, narrow_count, rows, LANES),
+                    lambda j, slots_ref: (j, 0, 0, 0),
                 )
             ],
             out_specs=pl.BlockSpec((D, LANES), lambda j, slots_ref: (0, j)),
         ),
-        cost_estimate=pl.CostEstimate(flops=0, bytes_accessed=4 * D * D, transcendentals=0),
+        cost_estimate=short,
         name="pick_merge",
     )(slots, weight_all)
 
@@ -400,11 +427,7 @@
             ],
         ),
         input_output_aliases={7 + k: k for k in range(len(held))},
-        cost_estimate=pl.CostEstimate(
-            flops=2 * 2 * count * count * LANES,
-            bytes_accessed=12 * count * LANES,
-            transcendentals=2 * count * count,
-        ),
+        cost_estimate=short,
         name="attend",
     )(slots, first, last, starts.reshape(1, count), packed, packed, packed, *held)
 
@@ -425,10 +448,16 @@
     tall_ref,
     log_ref,
     grad_ref,
-    *refs,
+    out_ref,
+    turned,
+    masked_q,
+    masked_g,
+    delta,
+    tall_q,
+    key_sum,
+    value_sum,
 ):
-    out_ref, turned, masked_q, masked_g, delta, tall_q, key_sum, value_sum = refs[-8:]
-    index = pl.program_id(0)
+    index = pl.program_id(1)
     count = query_ref.shape[0]
 
     def turn_back(field, rows):
@@ -497,7 +526,7 @@
     out_ref[key_rows, LANES : 2 * LANES] = turn_back(key_sum[...], key_rows).astype(jnp.bfloat16)
     out_ref[key_rows, 2 * LANES :] = value_sum[...].astype(jnp.bfloat16)
 
-    @pl.when(index == pl.num_programs(0) - 1)
+    @pl.when(index == pl.num_programs(1) - 1)
     def _():
         def finish(j, carry):
             rows = pl.ds(pl.multiple_of(j * block_k, block_k), block_k)
@@ -509,30 +538,28 @@
 
 
 def attend_back(
-    pair, packed, slots, last, end, starts, cosine, sine, tall, logs, grads,
-    heads_in, block_q, block_k, held,
+    packed, slots, last, end, starts, cosine, sine, tall, logs, grads, heads_in, block_q, block_k
 ):
     count, width = packed.shape
-    whole = pl.BlockSpec(memory_space=pl.ANY)
+    pairs = width // 3 // LANES
     return pl.pallas_call(
         partial(attend_back_kernel, block_q, block_k, heads_in),
         out_shape=jax.ShapeDtypeStruct((count, width), jnp.bfloat16),
         grid_spec=pltpu.PrefetchScalarGridSpec(
             num_scalar_prefetch=3,
-            grid=(count // block_k,),
+            grid=(pairs, count // block_k),
             in_specs=[
-                pl.BlockSpec((1, count), lambda i, *_: (0, 0)),
-                pl.BlockSpec((count, LANES), lambda i, *_: (0, 0)),
-                pl.BlockSpec((count, LANES), lambda i, *_: (0, 0)),
-                pl.BlockSpec((count, LANES), lambda i, *_: (0, 3 * pair)),
-                pl.BlockSpec((count, LANES), lambda i, *_: (0, 3 * pair + 1)),
-                pl.BlockSpec((count, LANES), lambda i, *_: (0, 3 * pair + 2)),
-                pl.BlockSpec((LANES, count), lambda i, *_: (pair, 0)),
-                pl.BlockSpec((1, 8, count), lambda i, *_: (pair, 0, 0)),
-                pl.BlockSpec((count, LANES), lambda i, *_: (0, pair)),
-            ]
-            + [whole] * len(held),
-            out_specs=pl.BlockSpec((count, 3 * LANES), lambda i, *_: (0, pair)),
+                pl.BlockSpec((1, count), lambda p, i, *_: (0, 0)),
+                pl.BlockSpec((count, LANES), lambda p, i, *_: (0, 0)),
+                pl.BlockSpec((count, LANES), lambda p, i, *_: (0, 0)),
+                pl.BlockSpec((count, LANES), lambda p, i, *_: (0, 3 * p)),
+                pl.BlockSpec((count, LANES), lambda p, i, *_: (0, 3 * p + 1)),
+                pl.BlockSpec((count, LANES), lambda p, i, *_: (0, 3 * p + 2)),
+                pl.BlockSpec((LANES, count), lambda p, i, *_: (p, 0)),
+                pl.BlockSpec((1, 8, count), lambda p, i, *_: (p, 0, 0)),
+                pl.BlockSpec((count, LANES), lambda p, i, *_: (0, p)),
+            ],
+            out_specs=pl.BlockSpec((count, 3 * LANES), lambda p, i, *_: (0, p)),
             scratch_shapes=[
                 pltpu.VMEM((LANES, count), jnp.bfloat16),
                 pltpu.VMEM((heads_in, count, LANES), jnp.bfloat16),
@@ -543,17 +570,12 @@
                 pltpu.VMEM((block_k, LANES), jnp.float32),
             ],
         ),
-        input_output_aliases={12 + k: k for k in range(len(held))},
         compiler_params=pltpu.CompilerParams(vmem_limit_bytes=60 << 20),
-        cost_estimate=pl.CostEstimate(
-            flops=5 * 2 * count * count * LANES,
-            bytes_accessed=20 * count * LANES,
-            transcendentals=2 * count * count,
-        ),
+        cost_estimate=short,
         name="attend_back",
     )(
         slots, last, end, starts.reshape(1, count), cosine, sine,
-        packed, packed, packed, tall, logs, grads, *held,
+        packed, packed, packed, tall, logs, grads,
     )
 
 
@@ -714,6 +736,43 @@
     return (weight - step_rate * (step_ratio + decay_coef * weight), new_first, new_second)
 
 
+def adam_kernel(scale_ref, grads_ref, *refs):
+    clip_factor, step_rate, first_scale, second_scale = [scale_ref[0, k] for k in range(4)]
+    for matrix in range(2):
+        weight = refs[3 * matrix][...]
+        gradient = grads_ref[0, matrix].astype(jnp.float32) * clip_factor
+        new_first = beta_first * refs[3 * matrix + 1][...] + (1.0 - beta_first) * gradient
+        new_second = (
+            beta_second * refs[3 * matrix + 2][...] + (1.0 - beta_second) * gradient * gradient
+        )
+        ratio = new_first * first_scale / (jnp.sqrt(new_second * second_scale) + adam_eps)
+        new_weight = weight - step_rate * (ratio + decay_rate * weight)
+        outs = refs[6 + 4 * matrix : 10 + 4 * matrix]
+        for out_ref, value in zip(outs, (new_weight, new_first, new_second)):
+            out_ref[...] = value
+        outs[3][...] = new_weight.astype(jnp.bfloat16)
+
+
+def adam_feed(scales, grads_all, *states):
+    count, matrices, rows, cols = grads_all.shape
+    block = pl.BlockSpec((rows, cols), lambda i: (i, 0))
+    full = jax.ShapeDtypeStruct((count * rows, cols), jnp.float32)
+    copy = jax.ShapeDtypeStruct((count * rows, cols), jnp.bfloat16)
+    return pl.pallas_call(
+        adam_kernel,
+        out_shape=(full, full, full, copy) * 2,
+        grid=(count,),
+        in_specs=[
+            pl.BlockSpec(memory_space=pltpu.SMEM),
+            pl.BlockSpec((1, matrices, rows, cols), lambda i: (i, 0, 0, 0)),
+        ]
+        + [block] * 6,
+        out_specs=(block,) * 8,
+        cost_estimate=short,
+        name="adam_feed",
+    )(scales, grads_all, *states)
+
+
 def shards(
     tokens,
     cotangent,
@@ -769,27 +828,41 @@
     weight_part = jnp.concatenate(
         [proj_weight.astype(jnp.bfloat16), merge_weight.astype(jnp.bfloat16)], axis=1
     )
-    weight_all = lax.all_gather(weight_part, ("narrow", "wide"), axis=0).reshape(
-        narrow_count, wide_count, shard_rows, -1
-    )
+    weight_rows = lax.all_gather(weight_part, "narrow", axis=0, tiled=True)
     up_slice = up_weight.astype(jnp.bfloat16)
     down_slice = down_weight.astype(jnp.bfloat16)
 
-    places = (
-        slots[:, None] * tok_rows + jnp.arange(tok_rows, dtype=jnp.int32)[None, :]
-    ).reshape(group_rows)
-    seq_start, unused = locate(lengths, places)
-    cosine, sine = rotary_tables(places - seq_start)
-    block_first = jnp.arange(narrow_count, dtype=jnp.int32) * tok_rows
-    first_start, unused = locate(lengths, block_first)
-    last_start, last_end = locate(lengths, block_first + (tok_rows - 1))
-
+    def wide_all(array):
+        return lax.all_gather(array, "wide", axis=0).reshape(
+            wide_count, narrow_count, shard_rows, -1
+        )
+
+    order = list(range(1, narrow_count)) + [0]
+    pairs = held_width // LANES
     token_blocks = [tokens]
     held = ()
     for slot in range(narrow_count - 1):
         moving = send_on(token_blocks[slot])
         held = feed(slot, narrow_count, token_blocks[slot], norm_params, up_slice, held)
-        moving, *held = meet(moving, *held)
+        moving, held = meet(moving, held)
+        if slot == 0:
+            lengths, slots, moving, weight_rows = meet(lengths, slots, moving, weight_rows)
+            proj_all = wide_all(weight_rows[:, :proj_cols])
+            merge_all = wide_all(weight_rows[:, proj_cols:])
+        if slot == 1 or narrow_count == 2:
+            places = (
+                slots[:, None] * tok_rows + jnp.arange(tok_rows, dtype=jnp.int32)[None, :]
+            ).reshape(group_rows)
+            seq_start, unused = locate(lengths, places)
+            cosine, sine = rotary_tables(places - seq_start)
+            block_first = jnp.arange(narrow_count, dtype=jnp.int32) * tok_rows
+            first_start, unused = locate(lengths, block_first)
+            last_start, last_end = locate(lengths, block_first + (tok_rows - 1))
+            moving, cosine, sine, first_start, last_start, last_end = meet(
+                moving, cosine, sine, first_start, last_start, last_end
+            )
+        elif slot == 2:
+            moving, down_slice = meet(moving, down_slice)
         token_blocks.append(moving)
     grad_first, last_block = meet(cotangent, token_blocks[-1])
     token_blocks[-1] = last_block
@@ -800,35 +873,23 @@
         narrow_count - 1, narrow_count, last_block, norm_params, up_slice, held
     )
     if direct:
-        proj_own = pick_proj(weight_all, span_index, own_width)
-        merge_turn = pick_merge(weight_all, slots, own_width)
+        proj_own = pick_proj(proj_all, span_index, own_width)
+        merge_turn = pick_merge(merge_all, slots, own_width)
     else:
-        turned_all = jnp.transpose(weight_all, (0, 2, 1, 3))
-        proj_copy = turned_all[..., :proj_cols].reshape(D, 3, narrow_count, own_width)
+        proj_copy = jnp.transpose(proj_all, (1, 2, 0, 3)).reshape(
+            D, 3, narrow_count, own_width
+        )
         proj_own = pad_lanes(
             lax.dynamic_index_in_dim(proj_copy, span_index, axis=2, keepdims=False), 2
         ).reshape(D, 3 * held_width)
-        merge_copy = turned_all[..., proj_cols:].reshape(narrow_count, own_width, D)
+        merge_copy = jnp.transpose(merge_all, (1, 2, 0, 3)).reshape(
+            narrow_count, own_width, D
+        )
         merge_turn = jnp.take(merge_copy, slots, axis=0).reshape(D, D)
+    merge_own = pad_lanes(merge_turn[:own_width], 0)
     packed = project(gathered, proj_own, cosine, sine)
-    moving, packed = meet(moving, packed)
+    moving, packed, activated, slope = meet(moving, packed, activated, slope)
     grad_blocks.append(moving)
-
-    pairs = held_width // LANES
-    attended_held = ()
-    for hop in range(2, max(narrow_count, pairs + 2)):
-        if hop < narrow_count:
-            moving = send_on(grad_blocks[-1])
-        if hop - 2 < pairs:
-            attended_held = attend(
-                hop - 2, packed, slots, first_start, last_start, seq_start,
-                heads_in, tok_rows, tok_rows, attended_held,
-            )
-        moving, *attended_held = meet(moving, *attended_held)
-        if hop < narrow_count:
-            grad_blocks.append(moving)
-    attended, tall, logs = attended_held
-    grads_all = jnp.concatenate(grad_blocks, axis=0)
 
     def down_term(slot):
         return dot_plain(rows_of(activated, slot), down_slice)
@@ -836,98 +897,149 @@
     def wide_sum(grad):
         return lax.psum_scatter(grad, "wide", scatter_dimension=0, tiled=True)
 
-    pieces = []
-    for ahead in range(narrow_count):
-        piece = rows_of(attended, (narrow_count - ahead) % narrow_count)[:, :own_width]
-        if ahead > 0:
-            piece = lax.ppermute(
-                piece,
-                "narrow",
-                [(i, (i + ahead) % narrow_count) for i in range(narrow_count)],
-            )
-        pieces.append(piece)
-
+    def attend_pair(pair, attended_held):
+        return attend(
+            pair, packed, slots, first_start, last_start, seq_start,
+            heads_in, tok_rows, tok_rows, attended_held,
+        )
+
+    def push_slot(slot, push_held):
+        return push(
+            slot, narrow_count, grad_blocks[slot], slope, down_slice, merge_own, push_held
+        )
+
+    attended_held = ()
+    push_held = ()
+    pushed = 0
     first_term = down_term(1).astype(jnp.bfloat16)
-    first_term, grads_all = meet(first_term, grads_all)
+    for hop in range(2, narrow_count):
+        moving = send_on(grad_blocks[-1])
+        if hop - 2 < pairs:
+            attended_held = attend_pair(hop - 2, attended_held)
+        for pushed in range(pushed, hop):
+            push_held = push_slot(pushed, push_held)
+        pushed = hop
+        moving, attended_held, push_held, first_term = meet(
+            moving, attended_held, push_held, first_term
+        )
+        grad_blocks.append(moving)
+    for pair in range(narrow_count - 2, pairs):
+        attended_held = attend_pair(pair, attended_held)
+    attended, tall, logs = attended_held
+
     moving = send_on(first_term)
-    hidden_grad = (dot_last(grads_all, down_slice) * slope).astype(jnp.bfloat16)
+    for slot in range(pushed, narrow_count):
+        push_held = push_slot(slot, push_held)
+    grads_all, hidden_grad, attended_grad = push_held
+    part_rows = D // wide_count
     down_grad = dot_first(activated, grads_all).astype(jnp.bfloat16)
     up_grad = dot_first(gathered, hidden_grad).astype(jnp.bfloat16)
-    attended_grad = pad_lanes(
-        dot_last(grads_all, merge_turn[:own_width]).astype(jnp.bfloat16), 1
-    )
-    moving, hidden_grad, attended_grad = meet(moving, hidden_grad, attended_grad)
-    mixed_held = ()
-    for hop in range(2, max(narrow_count, pairs + 2)):
-        if hop < narrow_count:
-            moving = send_on((moving.astype(jnp.float32) + down_term(hop)).astype(jnp.bfloat16))
-        if hop - 2 < pairs:
-            mixed_held = (
-                attend_back(
-                    hop - 2, packed, slots, last_start, last_end, seq_start, cosine, sine,
-                    tall, logs, attended_grad, heads_in, tok_rows, tok_rows, mixed_held,
-                ),
+    next_term = down_term(order[1])
+    pieces = [
+        rows_of(attended, (narrow_count - ahead) % narrow_count)[:, :own_width]
+        for ahead in range(narrow_count)
+    ]
+    moving, pieces, up_grad, down_grad, attended_grad, next_term = meet(
+        moving, pieces, up_grad, down_grad, attended_grad, next_term
+    )
+    feed_grad = jnp.concatenate(
+        [
+            up_grad.reshape(wide_count, part_rows, -1),
+            down_grad.reshape(wide_count, part_rows, -1),
+        ],
+        axis=1,
+    ).reshape(2 * D, -1)
+    feed_part = wide_sum(feed_grad)
+
+    def heads_back():
+        mixed = attend_back(
+            packed, slots, last_start, last_end, seq_start, cosine, sine,
+            tall, logs, attended_grad, heads_in, tok_rows, tok_rows,
+        )
+        proj_grad = dot_first(gathered, mixed).astype(jnp.bfloat16)
+        merge_grad = dot_first(grads_all, attended).astype(jnp.bfloat16)
+        if not direct:
+            proj_grad = proj_grad.reshape(D, 3, held_width)[:, :, :own_width].reshape(D, -1)
+            merge_grad = merge_grad[:, :own_width]
+        return (mixed, jnp.concatenate([proj_grad, merge_grad], axis=1))
+
+    for ahead in range(1, narrow_count):
+        pieces[ahead] = lax.ppermute(
+            pieces[ahead],
+            "narrow",
+            [(i, (i + ahead) % narrow_count) for i in range(narrow_count)],
+        )
+    terms = []
+    norm_part = jnp.zeros((2, D), jnp.float32)
+
+    def pull_more(count, mixed, norm_part):
+        for slot in order[len(terms) : len(terms) + count]:
+            term, sums = pull(slot, mixed, hidden_grad, proj_own, up_slice, token_blocks[slot])
+            terms.append(term)
+            norm_part = norm_part + sums
+        return norm_part
+
+    if narrow_count == 2:
+        mixed_grad, heads_grad = heads_back()
+        pieces, mixed_grad, heads_grad = meet(pieces, mixed_grad, heads_grad)
+    for place, slot in enumerate(order[1:-1]):
+        moving = send_on((moving.astype(jnp.float32) + next_term).astype(jnp.bfloat16))
+        next_term = down_term(order[place + 2])
+        if place == 0:
+            mixed_grad, heads_grad = heads_back()
+            moving, pieces, mixed_grad, heads_grad, next_term = meet(
+                moving, pieces, mixed_grad, heads_grad, next_term
             )
-        moving, *mixed_held = meet(moving, *mixed_held)
-    (mixed_grad,) = mixed_held
-    branch = moving.astype(jnp.float32) + down_term(0)
+            heads_part = wide_sum(heads_grad)
+        else:
+            norm_part = pull_more(4, mixed_grad, norm_part)
+            moving, terms, norm_part, next_term = meet(moving, terms, norm_part, next_term)
+        if slot == narrow_count - 1:
+            moving, feed_part = meet(moving, feed_part)
+    if narrow_count == 2:
+        heads_part = wide_sum(heads_grad)
+    norm_part = pull_more(narrow_count, mixed_grad, norm_part)
+    feed_all = lax.all_gather(feed_part, "wide", axis=0).reshape(
+        wide_count, 2, part_rows, -1
+    )
+
+    branch_moving = moving
+    moving = send_on(terms[0].astype(jnp.bfloat16))
+    branch = branch_moving.astype(jnp.float32) + next_term
     merged = dot_plain(jnp.concatenate(pieces, axis=1), merge_turn)
     unit_rows, inv_std = normalize(tokens)
     output_rows = tokens.astype(jnp.float32) + merged + branch
     layer_out = output_rows.astype(jnp.bfloat16)
 
-    terms = [None] * narrow_count
-    norm_part = None
-    for slot in list(range(1, narrow_count)) + [0]:
-        terms[slot], sums = pull(
-            slot, mixed_grad, hidden_grad, proj_own, up_slice, token_blocks[slot]
-        )
-        norm_part = sums if norm_part is None else norm_part + sums
-    moving = terms[1].astype(jnp.bfloat16)
-    for slot in list(range(2, narrow_count)) + [0]:
-        normed_grad = send_on(moving).astype(jnp.float32) + terms[slot]
-        moving = normed_grad.astype(jnp.bfloat16)
-    unit_grad = normed_grad * norm_params[0]
-    input_grad = cotangent.astype(jnp.float32) + inv_std * (
-        unit_grad
-        - jnp.mean(unit_grad, axis=1, keepdims=True)
-        - unit_rows * jnp.mean(unit_grad * unit_rows, axis=1, keepdims=True)
-    )
-
-    part_rows = D // wide_count
-    feed_part = wide_sum(
-        jnp.concatenate(
-            [
-                up_grad.reshape(wide_count, part_rows, -1),
-                down_grad.reshape(wide_count, part_rows, -1),
-            ],
-            axis=1,
-        ).reshape(2 * D, -1)
-    )
-    proj_grad = dot_first(gathered, mixed_grad).astype(jnp.bfloat16)
-    merge_grad = dot_first(grads_all, attended).astype(jnp.bfloat16)
-    if not direct:
-        proj_grad = proj_grad.reshape(D, 3, held_width)[:, :, :own_width].reshape(D, -1)
-        merge_grad = merge_grad[:, :own_width]
-    heads_part = wide_sum(jnp.concatenate([proj_grad, merge_grad], axis=1))
-    merge_block = heads_part[:, 3 * own_width :].T.astype(jnp.float32)
-
     def squares(array):
         value = array.astype(jnp.float32)
         return jnp.sum(value * value)
 
+    row_squares = [squares(output_rows), squares(merged), squares(branch)]
+    sent = None
+    for place in range(1, narrow_count - 1):
+        if place == 1:
+            moving, row_squares, norm_part = meet(moving, row_squares, norm_part)
+        elif place == narrow_count - 2:
+            moving, heads_part = meet(moving, heads_part)
+        sent = (moving.astype(jnp.float32) + terms[place]).astype(jnp.bfloat16)
+        if place < narrow_count - 2:
+            moving = send_on(sent)
+
     scalars = jnp.stack(
         [
             squares(heads_part) + squares(feed_part),
-            squares(output_rows),
-            squares(merged),
-            squares(branch),
         ]
+        + row_squares
     )
     parts = jnp.concatenate(
         [norm_part.reshape(2 * D // LANES, LANES), jnp.pad(scalars, (0, LANES - 4))[None, :]]
     )
     parts = jnp.pad(parts, ((0, 7), (0, 0)))
+    if sent is not None:
+        sent, parts = meet(sent, parts)
+        moving = send_on(sent)
+    merge_block = heads_part[:, 3 * own_width :].T.astype(jnp.float32)
     if direct:
         summed, proj_block = finish(
             parts, heads_part, narrow_count, wide_count, own_width, proj_cols
@@ -947,11 +1059,6 @@
     square_total = summed[2 * D // LANES, 0:1]
     output_squares = summed[2 * D // LANES, 1:2]
     branch_squares = summed[2 * D // LANES, 2:4]
-    feed_all = lax.all_gather(feed_part, "wide", axis=0).reshape(
-        wide_count, 2, part_rows, -1
-    ).astype(jnp.float32)
-    up_sum = feed_all[:, 0].reshape(up_weight.shape)
-    down_sum = feed_all[:, 1].reshape(down_weight.shape)
     grad_norm = jnp.sqrt(square_total + jnp.sum(norm_total * norm_total))
     clip_factor = jnp.minimum(1.0, math.sqrt(NPARAMS) / grad_norm)
     entry_count = wide_count * group_rows * D
@@ -992,25 +1099,37 @@
         first_fix,
         second_fix,
     )
-    new_up = adam_update(
-        up_weight,
-        up_first,
-        up_second,
-        up_sum * clip_factor,
-        matrix_rate * ramp,
-        decay_rate,
-        first_fix,
-        second_fix,
-    )
-    new_down = adam_update(
-        down_weight,
-        down_first,
-        down_second,
-        down_sum * clip_factor,
-        matrix_rate * ramp,
-        decay_rate,
-        first_fix,
-        second_fix,
+    if direct:
+        scales = jnp.stack(
+            [clip_factor[0], matrix_rate * ramp, 1.0 / first_fix, 1.0 / second_fix]
+        ).reshape(1, 4)
+        updated = adam_feed(
+            scales, feed_all, up_weight, up_first, up_second, down_weight, down_first, down_second
+        )
+        new_up, new_down = (updated[:4], updated[4:])
+    else:
+        feed_sums = feed_all.astype(jnp.float32)
+        new_up, new_down = [
+            adam_update(
+                *state,
+                feed_sums[:, matrix].reshape(state[0].shape) * clip_factor,
+                matrix_rate * ramp,
+                decay_rate,
+                first_fix,
+                second_fix,
+            )
+            for matrix, state in enumerate(
+                [(up_weight, up_first, up_second), (down_weight, down_first, down_second)]
+            )
+        ]
+        new_up, new_down = [new + (new[0].astype(jnp.bfloat16),) for new in (new_up, new_down)]
+    moving, new_up = meet(moving, new_up)
+    normed_grad = moving.astype(jnp.float32) + terms[-1]
+    unit_grad = normed_grad * norm_params[0]
+    input_grad = cotangent.astype(jnp.float32) + inv_std * (
+        unit_grad
+        - jnp.mean(unit_grad, axis=1, keepdims=True)
+        - unit_rows * jnp.mean(unit_grad * unit_rows, axis=1, keepdims=True)
     )
     return (
         layer_out,
@@ -1036,8 +1155,8 @@
         branch_norms,
         new_proj[0].astype(jnp.bfloat16),
         new_merge[0].astype(jnp.bfloat16),
-        new_up[0].astype(jnp.bfloat16),
-        new_down[0].astype(jnp.bfloat16),
+        new_up[3],
+        new_down[3],
     )
 
 

time: 538 us -> 486 us (0.903)
  waiting for transfers between devices: 163 us -> 105 us
  Pallas kernels: 176 us -> 223 us
  other arithmetic: 93.1 us -> 58 us
  matrix products: 59.1 us -> 37.3 us
  local copies, waits for them, and re-layouts: 11.7 us -> 19.4 us
    pallas_call x0 -> x5, Pallas kernels: none -> 41.3 us  [the longest x1 22 us: adam_feed(): pl.pallas_call(adam_kernel, out_shape=(full, full, full, copy) * 2, grid=...]
    ppermute x12, waiting for transfers between devices: 140 us -> 102 us  [send_on(): return lax.ppermute(array, 'narrow', onward)]
    convert_element_type x8 -> x5, other arithmetic: 47.1 us -> 10.3 us  [the longest x2 4.6 us: shards(): (moving.astype(jnp.float32) + next_term).astype(jnp.bfloat16)]
    ppermute x3, waiting for transfers between devices: 22.3 us -> 0.01 us  [shards(): lax.ppermute(pieces[ahead], 'narrow', [(i, (i + ahead) % narrow_count) fo...]
    dot_general x2 -> x0, matrix products: 12.1 us -> none  [dot_last(): lax.dot_general(left_side, right_side, (((1,), (1,)), ((), ())), preferre...]
    pallas_call x2, Pallas kernels: 28.4 us -> 40.5 us  [attend(): pl.pallas_call(partial(attend_kernel, block_q, block_k, heads_in), out_sh...]
    pallas_call x1, Pallas kernels: 42.6 us -> 31.9 us  [finish(): pl.pallas_call(partial(finish_kernel, narrow_count, wide_count, own_units...]
    dot_general x5, matrix products: 23.1 us -> 16.3 us  [dot_plain(): lax.dot_general(left_side, right_side, (((1,), (0,)), ((), ())), preferre...]
  transfers between devices with their start and end apart: 19 -> 21, of which waited for: 13 -> 8; matrix products, arithmetic and copies ran while one was open for 17% -> 20% of each run, Pallas kernels for 33% -> 47%
where the time goes in v2:
time: 486 us; the launch traced here: 477 us
  Pallas kernels  223 us (46%)
  waiting for transfers between devices  105 us (22%)
  other arithmetic  58 us (12%)
  matrix products  37.3 us (8%)
  between operations  21.9 us (5%)
  local copies, waits for them, and re-layouts  19.4 us (4%)
  starting transfers between devices  12.1 us (2%)
    ppermute x12, waiting for transfers between devices, send_on(): return lax.ppermute(array, 'narrow', onward)  102 us
    pallas_call x1, Pallas kernels, attend_back(): pl.pallas_call(partial(attend_back_kernel, block_q, block_k, heads_in), o...  43.1 us
    pallas_call x2, Pallas kernels, attend(): pl.pallas_call(partial(attend_kernel, block_q, block_k, heads_in), out_sh...  40.5 us
    pallas_call x1, Pallas kernels, finish(): pl.pallas_call(partial(finish_kernel, narrow_count, wide_count, own_units...  31.9 us
    pallas_call x4, Pallas kernels, pull(): pl.pallas_call(pull_kernel, out_shape=(jax.ShapeDtypeStruct((rows, depth)...  24.7 us
    pallas_call x4, Pallas kernels, feed(): pl.pallas_call(feed_kernel, out_shape=(jax.ShapeDtypeStruct((slots * rows...  22.6 us
    pallas_call x1, Pallas kernels, adam_feed(): pl.pallas_call(adam_kernel, out_shape=(full, full, full, copy) * 2, grid=...  22 us
    dot_general x4, matrix products, dot_first(): lax.dot_general(left_side, right_side, (((0,), (0,)), ((), ())), preferre...  21 us
  transfers between devices with their start and end apart: 21, of which 8 were waited for; matrix products, arithmetic and copies ran while one was open for 20% of the time, Pallas kernels for 47%

profile of v2, /device:TPU:0, one launch (start us, length us, event | category | flops | bytes accessed | tf_op | source)
XLA Modules:
  0.0 477.1 jit_solution(3302006335736399751)
XLA Ops:
  16.9 5.6 %feed.4 = (bf16[2048,1024]{1,0:T(8,128)(2,1)}, bf16[2048,1024]{1,0:T(8,128)(2,1)}, f32[2048,1024]{1,0:T(8,128)}) custom-call(bf16[512,1024]{1,0:T(8,128)(2,1)} %tokens_ref.3, f32[2,1024]{1,0:T(2,128)} %params_ref.7, bf16[1024,1024]{1,0:T(8,128)(2,1)} %convert_element_type.114.weight_ref.up_ref), custom_call_target="tpu_custom_call" | custom-call | tf_op jit(solution)/shard_map/feed/pallas_call | solution.py:140
  22.5 30.4 %collective-permute-done.tokens_ref = bf16[512,1024]{1,0:T(8,128)(2,1)S(1)} collective-permute-done((bf16[512,1024]{1,0:T(8,128)(2,1)}, bf16[512,1024]{1,0:T(8,128)(2,1)S(1)}, u32[]{:S(2)}, u32[]{:S(2)}) %collective-permute-start) | collective-permute-done | bytes 1048608 | tf_op jit(solution)/shard_map/ppermute | solution.py:822
  61.8 5.6 %feed.5 = (bf16[2048,1024]{1,0:T(8,128)(2,1)}, bf16[2048,1024]{1,0:T(8,128)(2,1)}, f32[2048,1024]{1,0:T(8,128)}) custom-call(bf16[512,1024]{1,0:T(8,128)(2,1)} %copy-done.7, f32[2,1024]{1,0:T(2,128)} %params_ref.7, bf16[1024,1024]{1,0:T(8,128)(2,1)} %convert_element_type.114.weight_ref.up_ref, ...), custom_call_target="tpu_custom_call", output_to_operand_aliasing={{0}: (3, {}), {1}: (4, {}), {2}: (5, {})} | custom-call | tf_op jit(solution)/shard_map/feed/pallas_call | solution.py:140
  67.6 5.6 %fusion.10 = (f32[2048,128]{1,0:T(8,128)}, f32[2048,128]{1,0:T(8,128)}) fusion(f32[128]{0:T(128)S(1)} %compare_select_fusion.2, f32[128]{0:T(128)S(1)} %mul.211, f32[2048]{0:T(1024)S(1)} %subtract_convert_fusion), kind=kLoop, calls=%fused_computation.31 | loop fusion | flops 524288 | bytes 2106368 | tf_op jit(solution)/shard_map/mul | solution.py:69
  73.1 13.5 %collective-permute-done.1.tokens_ref = bf16[512,1024]{1,0:T(8,128)(2,1)S(1)} collective-permute-done((bf16[512,1024]{1,0:T(8,128)(2,1)S(1)}, bf16[512,1024]{1,0:T(8,128)(2,1)S(1)}, u32[]{:S(2)}, u32[]{:S(2)}) %collective-permute-start.1) | collective-permute-done | bytes 1048608 | tf_op jit(solution)/shard_map/ppermute | solution.py:822
  90.9 5.7 %feed.6 = (bf16[2048,1024]{1,0:T(8,128)(2,1)}, bf16[2048,1024]{1,0:T(8,128)(2,1)}, f32[2048,1024]{1,0:T(8,128)}) custom-call(bf16[512,1024]{1,0:T(8,128)(2,1)} %copy-done.8, f32[2,1024]{1,0:T(2,128)} %params_ref.7, bf16[1024,1024]{1,0:T(8,128)(2,1)} %convert_element_type.114.weight_ref.up_ref, ...), custom_call_target="tpu_custom_call", output_to_operand_aliasing={{0}: (3, {}), {1}: (4, {}), {2}: (5, {})} | custom-call | tf_op jit(solution)/shard_map/feed/pallas_call | solution.py:140
  96.6 16.0 %collective-permute-done.2.tokens_ref = bf16[512,1024]{1,0:T(8,128)(2,1)S(1)} collective-permute-done((bf16[512,1024]{1,0:T(8,128)(2,1)S(1)}, bf16[512,1024]{1,0:T(8,128)(2,1)S(1)}, u32[]{:S(2)}, u32[]{:S(2)}) %collective-permute-start.2) | collective-permute-done | bytes 1048608 | tf_op jit(solution)/shard_map/ppermute | solution.py:822
  113.6 5.7 %feed.7 = (bf16[2048,1024]{1,0:T(8,128)(2,1)}, bf16[2048,1024]{1,0:T(8,128)(2,1)}, f32[2048,1024]{1,0:T(8,128)}) custom-call(bf16[512,1024]{1,0:T(8,128)(2,1)} %copy-done.9, f32[2,1024]{1,0:T(2,128)} %params_ref.7, bf16[1024,1024]{1,0:T(8,128)(2,1)} %convert_element_type.114.weight_ref.up_ref, ...), custom_call_target="tpu_custom_call", output_to_operand_aliasing={{0}: (3, {}), {1}: (4, {}), {2}: (5, {})} | custom-call | tf_op jit(solution)/shard_map/feed/pallas_call | solution.py:140
  124.0 8.2 %project.1.query_ref.key_ref.value_ref = bf16[2048,768]{1,0:T(8,128)(2,1)} custom-call(bf16[2048,1024]{1,0:T(8,128)(2,1)} %get-tuple-element.187.rows_ref, bf16[1024,768]{1,0:T(8,128)(2,1)} %pick_proj.1.weight_ref.proj_ref, f32[2048,128]{1,0:T(8,128)} %get-tuple-element.189.cos_ref, f32[2048,128]{1,0:T(8,128)} %get-tuple-element.190.sin_ref), custom_call_target="tpu_custom_call" | custom-call | tf_op jit(solution)/shard_map/project/pallas_call | solution.py:99
  132.1 5.8 %collective-permute-done.3.grad_ref = bf16[512,1024]{1,0:T(8,128)(2,1)} collective-permute-done((bf16[512,1024]{1,0:T(8,128)(2,1)S(1)}, bf16[512,1024]{1,0:T(8,128)(2,1)}, u32[]{:S(2)}, u32[]{:S(2)}) %collective-permute-start.3) | collective-permute-done | bytes 1048608 | tf_op jit(solution)/shard_map/ppermute | solution.py:822
  138.5 6.4 %pick_merge.1 = bf16[1024,1024]{1,0:T(8,128)(2,1)} custom-call(s32[4]{0:T(128)} %copy-done.32, bf16[8,4,256,128]{3,2,1,0:T(8,128)(2,1)} %bitcast.55), custom_call_target="tpu_custom_call" | custom-call | tf_op jit(solution)/shard_map/pick_merge/pallas_call | solution.py:284
  156.3 20.3 %attend.2 = (bf16[2048,256]{1,0:T(8,128)(2,1)}, f32[256,2048]{1,0:T(8,128)}, f32[2,8,2048]{2,1,0:T(8,128)}) custom-call(s32[4]{0:T(128)} %copy-done.32, s32[4]{0:T(128)} %select_reduce_fusion.3.first_ref, s32[4]{0:T(128)} %get-tuple-element.195.last_ref, s32[1,2048]{1,0:T(1,128)} %bitcast.58, bf16[2048,768]{1,0:T(8,128)(2,1)} %project.1.query_ref.key_ref.value_ref, ...), custom_call_target="tpu_custom_call" | custom-call | tf_op jit(solution)/shard_map/attend/pallas_call | solution.py:400
  183.8 20.2 %attend.3 = (bf16[2048,256]{1,0:T(8,128)(2,1)}, f32[256,2048]{1,0:T(8,128)}, f32[2,8,2048]{2,1,0:T(8,128)}) custom-call(s32[4]{0:T(128)} %copy-done.32, s32[4]{0:T(128)} %select_reduce_fusion.3.first_ref, s32[4]{0:T(128)} %get-tuple-element.195.last_ref, s32[1,2048]{1,0:T(1,128)} %bitcast.59, ...), custom_call_target="tpu_custom_call", output_to_operand_aliasing={{0}: (7, {}), {1}: (8, {}), {2}: (9, {})} | custom-call | tf_op jit(solution)/shard_map/attend/pallas_call | solution.py:400
  215.4 8.2 %convolution_convert_fusion.1 = bf16[1024,1024]{1,0:T(8,128)(2,1)S(1)} fusion(bf16[2048,1024]{1,0:T(8,128)(2,1)} %get-tuple-element.187.rows_ref, bf16[2048,1024]{1,0:T(8,128)(2,1)} %get-tuple-element.229.hidden_ref), kind=kOutput, calls=%fused_computation.25 | convolution fusion | flops 4296015872 | bytes 10485760 | tf_op jit(solution)/shard_map/dot_general | solution.py:45
  251.0 43.1 %attend_back.1.mixed_ref = bf16[2048,768]{1,0:T(8,128)(2,1)} custom-call(s32[4]{0:T(128)} %copy-done.32, s32[4]{0:T(128)} %get-tuple-element.195.last_ref, s32[4]{0:T(128)} %get-tuple-element.238.end_ref, s32[1,2048]{1,0:T(1,128)} %bitcast.60, f32[2048,128]{1,0:T(8,128)} %get-tuple-element.189.cos_ref, f32[2048,128]{1,0:T(8,128)} %get-tuple-element.190.sin_ref, ...), custom_call_target="tpu_custom_call" | custom-call | tf_op jit(solution)/shard_map/attend_back/pallas_call | solution.py:545
  294.1 6.7 %convolution_convert_fusion.2 = bf16[1024,768]{1,0:T(8,128)(2,1)S(1)} fusion(bf16[2048,1024]{1,0:T(8,128)(2,1)} %get-tuple-element.187.rows_ref, bf16[2048,768]{1,0:T(8,128)(2,1)} %attend_back.1.mixed_ref), kind=kOutput, calls=%fused_computation.26 | convolution fusion | flops 3222011904 | bytes 8912896 | tf_op jit(solution)/shard_map/dot_general | solution.py:45
  310.7 6.3 %pull.4 = (f32[512,1024]{1,0:T(8,128)}, f32[2,1024]{1,0:T(2,128)}) custom-call(bf16[2048,768]{1,0:T(8,128)(2,1)} %attend_back.1.mixed_ref, bf16[2048,1024]{1,0:T(8,128)(2,1)} %get-tuple-element.229.hidden_ref, bf16[1024,768]{1,0:T(8,128)(2,1)} %pick_proj.1.weight_ref.proj_ref, bf16[1024,1024]{1,0:T(8,128)(2,1)} %convert_element_type.114.weight_ref.up_ref, ...), custom_call_target="tpu_custom_call" | custom-call | tf_op jit(solution)/shard_map/pull/pallas_call | solution.py:225
  317.0 6.1 %pull.5 = (f32[512,1024]{1,0:T(8,128)}, f32[2,1024]{1,0:T(2,128)}) custom-call(bf16[2048,768]{1,0:T(8,128)(2,1)} %attend_back.1.mixed_ref, bf16[2048,1024]{1,0:T(8,128)(2,1)} %get-tuple-element.229.hidden_ref, bf16[1024,768]{1,0:T(8,128)(2,1)} %pick_proj.1.weight_ref.proj_ref, bf16[1024,1024]{1,0:T(8,128)(2,1)} %convert_element_type.114.weight_ref.up_ref, ...), custom_call_target="tpu_custom_call" | custom-call | tf_op jit(solution)/shard_map/pull/pallas_call | solution.py:225
  323.1 6.1 %pull.6 = (f32[512,1024]{1,0:T(8,128)}, f32[2,1024]{1,0:T(2,128)}) custom-call(bf16[2048,768]{1,0:T(8,128)(2,1)} %attend_back.1.mixed_ref, bf16[2048,1024]{1,0:T(8,128)(2,1)} %get-tuple-element.229.hidden_ref, bf16[1024,768]{1,0:T(8,128)(2,1)} %pick_proj.1.weight_ref.proj_ref, bf16[1024,1024]{1,0:T(8,128)(2,1)} %convert_element_type.114.weight_ref.up_ref, ...), custom_call_target="tpu_custom_call" | custom-call | tf_op jit(solution)/shard_map/pull/pallas_call | solution.py:225
  329.2 6.2 %pull.7 = (f32[512,1024]{1,0:T(8,128)}, f32[2,1024]{1,0:T(2,128)}) custom-call(bf16[2048,768]{1,0:T(8,128)(2,1)} %attend_back.1.mixed_ref, bf16[2048,1024]{1,0:T(8,128)(2,1)} %get-tuple-element.229.hidden_ref, bf16[1024,768]{1,0:T(8,128)(2,1)} %pick_proj.1.weight_ref.proj_ref, bf16[1024,1024]{1,0:T(8,128)(2,1)} %convert_element_type.114.weight_ref.up_ref, ...), custom_call_target="tpu_custom_call" | custom-call | tf_op jit(solution)/shard_map/pull/pallas_call | solution.py:225
  345.4 17.0 %collective-permute-done.12 = bf16[512,1024]{1,0:T(8,128)(2,1)S(1)} collective-permute-done((bf16[512,1024]{1,0:T(8,128)(2,1)S(1)}, bf16[512,1024]{1,0:T(8,128)(2,1)S(1)}, u32[]{:S(2)}, u32[]{:S(2)}) %collective-permute-start.12) | collective-permute-done | bytes 1048608 | tf_op jit(solution)/shard_map/ppermute | solution.py:822
  371.4 14.3 %collective-permute-done.13 = bf16[512,1024]{1,0:T(8,128)(2,1)} collective-permute-done((bf16[512,1024]{1,0:T(8,128)(2,1)}, bf16[512,1024]{1,0:T(8,128)(2,1)}, u32[]{:S(2)}, u32[]{:S(2)}) %collective-permute-start.13) | collective-permute-done | bytes 1048608 | tf_op jit(solution)/shard_map/ppermute | solution.py:822
  394.7 31.9 %finish.1 = (f32[24,128]{1,0:T(8,128)}, bf16[256,384]{1,0:T(8,128)(2,1)}) custom-call(f32[24,128]{1,0:T(8,128)} %select_maximum_fusion.refs_0_, bf16[128,1024]{1,0:T(8,128)(2,1)} %reduce-scatter.5.cloned.1.call-done.refs_1_), custom_call_target="tpu_custom_call" | custom-call | tf_op jit(solution)/shard_map/finish/pallas_call | solution.py:719
  439.9 22.0 %adam_feed.1 = (f32[1024,1024]{1,0:T(8,128)}, f32[1024,1024]{1,0:T(8,128)}, f32[1024,1024]{1,0:T(8,128)}, bf16[1024,1024]{1,0:T(8,128)(2,1)}, f32[1024,1024]{1,0...) custom-call(f32[1,4]{1,0:T(1,128)} %maximum_bitcast_fusion.scale_ref, ...), custom_call_target="tpu_custom_call" | custom-call | tf_op jit(solution)/shard_map/adam_feed/pallas_call | solution.py:761
  (212 shorter events, 138.4 us)
Async XLA Ops:
  7.2 48.5 %all-gather.8.cloned.1.call-start = ((), (), s32[]{:S(2)}) async-start(), calls=%async_computation.2 | async-start | bytes 1310720 | tf_op jit(solution)/shard_map/all_gather | solution.py:831
  9.9 109.4 %all-gather.10.cloned.1.call-start = ((), (), s32[]{:S(2)}) async-start(), calls=%async_computation.5 | async-start | bytes 7077888 | tf_op jit(solution)/shard_map/all_gather | solution.py:836
  10.0 42.9 %collective-permute-start = (bf16[512,1024]{1,0:T(8,128)(2,1)}, bf16[512,1024]{1,0:T(8,128)(2,1)S(1)}, u32[]{:S(2)}, u32[]{:S(2)}) collective-permute-start(bf16[512,1024]{1,0:T(8,128)(2,1)} %tokens_ref.3), channel_id=1, source_target_pairs={{0,1},{1,2},{2,3},{3,0},{4,5},{5,6},{6,7},{7,4},{8,9},{9,10},{10,1... | collective-permute-start | bytes 3145736 | tf_op jit(solution)/shard_map/ppermute | solution.py:822
  22.5 44.9 %copy-start.32 = (s32[4]{0:T(128)}, s32[4]{0:T(128)S(1)}, u32[]{:S(2)}) copy-start(s32[4]{0:T(128)S(1)} %compare_select_fusion.slots_ref) | copy-start | bytes 52
  57.8 80.6 %all-gather.12.cloned.1.call-start = ((), (), s32[]{:S(2)}) async-start(), calls=%async_computation.6 | async-start | bytes 2359296 | tf_op jit(solution)/shard_map/all_gather | solution.py:836
  59.8 26.9 %collective-permute-start.1 = (bf16[512,1024]{1,0:T(8,128)(2,1)S(1)}, bf16[512,1024]{1,0:T(8,128)(2,1)S(1)}, u32[]{:S(2)}, u32[]{:S(2)}) collective-permute-start(bf16[512,1024]{1,0:T(8,128)(2,1)S(1)} %collective-permute-done.tokens_ref), channel_id=1, source_target_pairs={{0,1},{1,2},{2,3},{3,0},{4,5},{5,6},{6,7},{7,4},{8,9},{9,10},{10,1... | collective-permute-start | bytes 3145736 | tf_op jit(solution)/shard_map/ppermute | solution.py:822
  60.3 276.7 %reduce-scatter.3.cloned.1.call-start = ((), (), s32[]{:S(2)}) async-start(), calls=%async_computation.3 | async-start | bytes 4718592 | tf_op jit(solution)/shard_map/reduce_scatter | solution.py:898
  86.6 26.0 %collective-permute-start.2 = (bf16[512,1024]{1,0:T(8,128)(2,1)S(1)}, bf16[512,1024]{1,0:T(8,128)(2,1)S(1)}, u32[]{:S(2)}, u32[]{:S(2)}) collective-permute-start(bf16[512,1024]{1,0:T(8,128)(2,1)S(1)} %collective-permute-done.1.tokens_ref), channel_id=1, source_target_pairs={{0,1},{1,2},{2,3},{3,0},{4,5},{5,6},{6,7},{7,4},{8,9},{9,10},{10,1... | collective-permute-start | bytes 3145736 | tf_op jit(solution)/shard_map/ppermute | solution.py:822
  112.6 25.3 %collective-permute-start.3 = (bf16[512,1024]{1,0:T(8,128)(2,1)S(1)}, bf16[512,1024]{1,0:T(8,128)(2,1)}, u32[]{:S(2)}, u32[]{:S(2)}) collective-permute-start(bf16[512,1024]{1,0:T(8,128)(2,1)S(1)} %copy-done.11), channel_id=1, source_target_pairs={{0,1},{1,2},{2,3},{3,0},{4,5},{5,6},{6,7},{7,4},{8,9},{9,10},{10,1... | collective-permute-start | bytes 3145736 | tf_op jit(solution)/shard_map/ppermute | solution.py:822
  137.9 42.1 %collective-permute-start.4 = (bf16[512,1024]{1,0:T(8,128)(2,1)}, bf16[512,1024]{1,0:T(8,128)(2,1)}, u32[]{:S(2)}, u32[]{:S(2)}) collective-permute-start(bf16[512,1024]{1,0:T(8,128)(2,1)} %collective-permute-done.3.grad_ref), channel_id=1, source_target_pairs={{0,1},{1,2},{2,3},{3,0},{4,5},{5,6},{6,7},{7,4},{8,9},{9,10},{10,1... | collective-permute-start | bytes 3145736 | tf_op jit(solution)/shard_map/ppermute | solution.py:822
  180.0 28.9 %collective-permute-start.5 = (bf16[512,1024]{1,0:T(8,128)(2,1)}, bf16[512,1024]{1,0:T(8,128)(2,1)}, u32[]{:S(2)}, u32[]{:S(2)}) collective-permute-start(bf16[512,1024]{1,0:T(8,128)(2,1)} %collective-permute-done.4.grad_ref), channel_id=1, source_target_pairs={{0,1},{1,2},{2,3},{3,0},{4,5},{5,6},{6,7},{7,4},{8,9},{9,10},{10,1... | collective-permute-start | bytes 3145736 | tf_op jit(solution)/shard_map/ppermute | solution.py:822
  209.0 24.5 %collective-permute-start.6 = (bf16[512,1024]{1,0:T(8,128)(2,1)S(1)}, bf16[512,1024]{1,0:T(8,128)(2,1)S(1)}, u32[]{:S(2)}, u32[]{:S(2)}) collective-permute-start(bf16[512,1024]{1,0:T(8,128)(2,1)S(1)} %copy-done.38), channel_id=1, source_target_pairs={{0,1},{1,2},{2,3},{3,0},{4,5},{5,6},{6,7},{7,4},{8,9},{9,10},{10,1... | collective-permute-start | bytes 3145736 | tf_op jit(solution)/shard_map/ppermute | solution.py:822
  236.0 135.4 %reduce-scatter.5.cloned.1.call-start = ((), (), s32[]{:S(2)}) async-start(), calls=%async_computation.4 | async-start | bytes 2359296 | tf_op jit(solution)/shard_map/reduce_scatter | solution.py:898
  242.9 59.6 %collective-permute-start.7 = (bf16[512,1024]{1,0:T(8,128)(2,1)}, bf16[512,1024]{1,0:T(8,128)(2,1)}, u32[]{:S(2)}, u32[]{:S(2)}) collective-permute-start(bf16[512,1024]{1,0:T(8,128)(2,1)} %add_convert_fusion.3), channel_id=1, source_target_pairs={{0,1},{1,2},{2,3},{3,0},{4,5},{5,6},{6,7},{7,4},{8,9},{9,10},{10,1... | collective-permute-start | bytes 3145736 | tf_op jit(solution)/shard_map/ppermute | solution.py:822
  245.9 56.5 %collective-permute-start.8 = (bf16[512,256]{1,0:T(8,128)(2,1)}, bf16[512,256]{1,0:T(8,128)(2,1)S(1)}, u32[]{:S(2)}, u32[]{:S(2)}) collective-permute-start(bf16[512,256]{1,0:T(8,128)(2,1)} %get-tuple-element.235), channel_id=1, source_target_pairs={{0,1},{1,2},{2,3},{3,0},{4,5},{5,6},{6,7},{7,4},{8,9},{9,10},{10,1... | collective-permute-start | bytes 786440 | tf_op jit(solution)/shard_map/ppermute | solution.py:967
  246.8 55.6 %collective-permute-start.9 = (bf16[512,256]{1,0:T(8,128)(2,1)}, bf16[512,256]{1,0:T(8,128)(2,1)S(1)}, u32[]{:S(2)}, u32[]{:S(2)}) collective-permute-start(bf16[512,256]{1,0:T(8,128)(2,1)} %get-tuple-element.236), channel_id=1, source_target_pairs={{0,2},{1,3},{2,0},{3,1},{4,6},{5,7},{6,4},{7,5},{8,10},{9,11},{10,... | collective-permute-start | bytes 786440 | tf_op jit(solution)/shard_map/ppermute | solution.py:967
  248.7 53.8 %collective-permute-start.10 = (bf16[512,256]{1,0:T(8,128)(2,1)}, bf16[512,256]{1,0:T(8,128)(2,1)S(1)}, u32[]{:S(2)}, u32[]{:S(2)}) collective-permute-start(bf16[512,256]{1,0:T(8,128)(2,1)} %get-tuple-element.237), channel_id=1, source_target_pairs={{0,3},{1,0},{2,1},{3,2},{4,7},{5,4},{6,5},{7,6},{8,11},{9,8},{10,9... | collective-permute-start | bytes 786440 | tf_op jit(solution)/shard_map/ppermute | solution.py:967
  302.5 137.3 %all-gather.14.cloned.1.call-start = ((), (), s32[]{:S(2)}) async-start(), calls=%async_computation.7 | async-start | bytes 4718592 | tf_op jit(solution)/shard_map/all_gather | solution.py:1002
  306.6 30.4 %collective-permute-start.11 = (bf16[512,1024]{1,0:T(8,128)(2,1)}, bf16[512,1024]{1,0:T(8,128)(2,1)S(1)}, u32[]{:S(2)}, u32[]{:S(2)}) collective-permute-start(bf16[512,1024]{1,0:T(8,128)(2,1)} %add_convert_fusion.2), channel_id=1, source_target_pairs={{0,1},{1,2},{2,3},{3,0},{4,5},{5,6},{6,7},{7,4},{8,9},{9,10},{10,1... | collective-permute-start | bytes 3145736 | tf_op jit(solution)/shard_map/ppermute | solution.py:822
  339.8 22.6 %collective-permute-start.12 = (bf16[512,1024]{1,0:T(8,128)(2,1)S(1)}, bf16[512,1024]{1,0:T(8,128)(2,1)S(1)}, u32[]{:S(2)}, u32[]{:S(2)}) collective-permute-start(bf16[512,1024]{1,0:T(8,128)(2,1)S(1)} %convert_element_type.134), channel_id=1, source_target_pairs={{0,1},{1,2},{2,3},{3,0},{4,5},{5,6},{6,7},{7,4},{8,9},{9,10},{10,1... | collective-permute-start | bytes 3145736 | tf_op jit(solution)/shard_map/ppermute | solution.py:822
  363.7 22.0 %collective-permute-start.13 = (bf16[512,1024]{1,0:T(8,128)(2,1)}, bf16[512,1024]{1,0:T(8,128)(2,1)}, u32[]{:S(2)}, u32[]{:S(2)}) collective-permute-start(bf16[512,1024]{1,0:T(8,128)(2,1)} %add_convert_fusion.1), channel_id=1, source_target_pairs={{0,1},{1,2},{2,3},{3,0},{4,5},{5,6},{6,7},{7,4},{8,9},{9,10},{10,1... | collective-permute-start | bytes 3145736 | tf_op jit(solution)/shard_map/ppermute | solution.py:822
  394.6 43.9 %copy-start.18 = (f32[256,384]{1,0:T(8,128)S(1)}, f32[256,384]{1,0:T(8,128)}, u32[]{:S(2)}) copy-start(f32[256,384]{1,0:T(8,128)} %param.26) | copy-start | bytes 1179652
  394.6 43.9 %copy-start.24 = (f32[256,384]{1,0:T(8,128)S(1)}, f32[256,384]{1,0:T(8,128)}, u32[]{:S(2)}) copy-start(f32[256,384]{1,0:T(8,128)} %param.28) | copy-start | bytes 1179652
  394.6 67.2 %collective-permute-start.14 = (bf16[512,1024]{1,0:T(8,128)(2,1)}, bf16[512,1024]{1,0:T(8,128)(2,1)}, u32[]{:S(2)}, u32[]{:S(2)}) collective-permute-start(bf16[512,1024]{1,0:T(8,128)(2,1)} %add_convert_fusion), channel_id=1, source_target_pairs={{0,1},{1,2},{2,3},{3,0},{4,5},{5,6},{6,7},{7,4},{8,9},{9,10},{10,1... | collective-permute-start | bytes 3145736 | tf_op jit(solution)/shard_map/ppermute | solution.py:822
  (43 other events, 457.2 us)
Sparse Core Ops, SparseCore 0:
  10.2 45.5 all-gather.7
  58.2 44.5 all-gather.9
  105.2 27.8 all-gather.11
  236.1 49.8 reduce-scatter.2
  302.6 38.7 reduce-scatter.4
  343.2 36.5 all-gather.13
